TPU v7x, 32 devices: a whole 2x2x4 slice. The times are simulated.
32 devices in a mesh: grp: 4 (over x, core), blk: 8 (over z, y).
Axes of the slice: x: 2, y: 2, z: 4, core: 2. Of those that a mesh axis runs over, the one named last changes fastest.
Arguments:
- targets: float32 [16, 262144], P('blk', 'grp'), may hold values from -6 to 6
- sources: float32 [32, 262144], P(('grp', 'blk')), may hold values from -6 to 6
- occupation: int32 [32], P(('grp', 'blk')), may hold values from 1 to 2
- offsets: int32 [4], replicated, may hold values from 0 to 7, as said below
Outputs:
- exchange: float32 [16, 262144], P('blk', 'grp')
Inputs may be any that keep to these rules, and one draw needn't show every extreme that they name: The groups' offsets are distinct and the largest is 7.
All inputs are finite; a program needn't handle non-finite values.
Results may differ from a plain program's by a relative error of at most 0.0003.
Values sent between devices are 32-bit elements; how exact they have to be, the bound alone decides.
A program may use at most 128 MiB of HBM per device.

v0:
```python
import math

import jax
import jax.numpy as jnp
from jax import lax
from jax.sharding import PartitionSpec as P

NG = 64
STOPS = 4


box_length = 16.0
screen_square = 0.25


def shifted(block, axis, distance):
    devices = range(lax.axis_size(axis))
    route = [((i - distance) % len(devices), i) for i in devices]
    return lax.ppermute(block, axis, route)


def screened_kernel(grid_size):
    counter = jnp.arange(grid_size, dtype=jnp.int32)
    signed_freq = jnp.where(counter < grid_size // 2, counter, counter - grid_size).astype(
        jnp.float32
    )
    wave_number = 2.0 * math.pi * signed_freq / box_length
    wave_square = wave_number * wave_number
    summed = wave_square[:, None, None] + wave_square[None, :, None] + wave_square[None, None, :]
    return 4.0 * math.pi / (summed + screen_square)


def dft_table(grid_size, sign_value, factor):
    counter = jnp.arange(grid_size, dtype=jnp.int32)
    product = counter[:, None] * counter[None, :] % grid_size
    phase_angle = 2.0 * math.pi * product.astype(jnp.float32) / grid_size
    cosine = jnp.cos(phase_angle) * factor
    sine_part = jnp.sin(phase_angle) * factor
    upper_rows = jnp.stack([cosine, -sign_value * sine_part], axis=1)
    lower_rows = jnp.stack([sign_value * sine_part, cosine], axis=1)
    return jnp.stack([upper_rows, lower_rows], axis=0)


def transform(grid_field, dft_matrix):
    for repeat_index in range(3):
        grid_field = jnp.einsum(
            "qmpa,zpabc->zqbcm", dft_matrix, grid_field, precision=lax.Precision.HIGHEST
        )
    return grid_field


def exchange_terms(target_rows, source_rows, kernel_grid, forward_table, inverse_table):
    target_count, cell_count = target_rows.shape
    source_count = source_rows.shape[0]
    density = (target_rows[:, None, :] * source_rows[None, :, :]).reshape(
        target_count * source_count, NG, NG, NG
    )
    half_count = density.shape[0] // 2
    packed = jnp.stack([density[:half_count], density[half_count:]], axis=1)
    both_parts = transform(transform(packed, forward_table) * kernel_grid, inverse_table)
    potential = jnp.concatenate([both_parts[:, 0], both_parts[:, 1]], axis=0)
    potential = potential.reshape(target_count, source_count, cell_count)
    return jnp.sum(potential * source_rows[None, :, :], axis=1)


def local(targets, sources, occupation, offsets):
    whole_targets = lax.all_gather(targets, "grp", axis=1, tiled=True)
    scaled = sources * jnp.sqrt(occupation.astype(jnp.float32) * 0.5)[:, None]
    group_offset = lax.dynamic_index_in_dim(offsets, lax.axis_index("grp"), 0, keepdims=False)
    carried = scaled
    for bit_number in range(lax.axis_size("blk").bit_length() - 1):
        moved_rows = shifted(carried, "blk", 1 << bit_number)
        carried = jnp.where(group_offset // (1 << bit_number) % 2 == 1, moved_rows, carried)
    kernel_grid = screened_kernel(NG)
    forward_table = dft_table(NG, -1.0, 1.0)
    inverse_table = dft_table(NG, 1.0, 1.0 / NG)
    accumulated = jnp.zeros(whole_targets.shape, jnp.float32)
    visiting = carried
    for stop_index in range(STOPS):
        if stop_index > 0:
            visiting = shifted(visiting, "blk", 1)
        accumulated = accumulated + exchange_terms(
            whole_targets, visiting, kernel_grid, forward_table, inverse_table
        )
    summed = lax.psum_scatter(accumulated, "grp", scatter_dimension=1, tiled=True)
    return -summed


def solution(mesh):
    in_specs = (P("blk", "grp"), P(("grp", "blk"), None), P(("grp", "blk")), P())
    out_specs = P("blk", "grp")
    return jax.shard_map(local, mesh=mesh, in_specs=in_specs, out_specs=out_specs, check_vma=False)
```

profile of v0, /device:TPU:0, one launch (start us, length us, event | category | flops | bytes accessed | tf_op | source)
XLA Modules:
  0.0 597.1 jit_solution(14541214707635236395)
XLA Ops:
  9.0 3.0 collective-permute-start
  15.5 22.8 %collective-permute-done = f32[1,262144]{1,0:T(1,128)S(1)} collective-permute-done((f32[1,262144]{1,0:T(1,128)S(1)}, f32[1,262144]{1,0:T(1,128)S(1)}, u32[]{:S(2)}, u32[]{:S(2)}) %collective-permute-start) | collective-permute-done | bytes 1048608 | tf_op jit(solution)/shard_map/ppermute | solution.py:19
  38.3 2.2 broadcast_select_fusion
  41.2 25.4 %collective-permute-done.1 = f32[1,262144]{1,0:T(1,128)S(1)} collective-permute-done((f32[1,262144]{1,0:T(1,128)S(1)}, f32[1,262144]{1,0:T(1,128)S(1)}, u32[]{:S(2)}, u32[]{:S(2)}) %collective-permute-start.1) | collective-permute-done | bytes 1048608 | tf_op jit(solution)/shard_map/ppermute | solution.py:19
  67.9 45.0 %collective-permute-done.2 = f32[1,262144]{1,0:T(1,128)S(1)} collective-permute-done((f32[1,262144]{1,0:T(1,128)S(1)}, f32[1,262144]{1,0:T(1,128)S(1)}, u32[]{:S(2)}, u32[]{:S(2)}) %collective-permute-start.2) | collective-permute-done | bytes 1048608 | tf_op jit(solution)/shard_map/ppermute | solution.py:19
  114.1 27.7 %collective-permute-done.3 = f32[1,262144]{1,0:T(1,128)S(1)} collective-permute-done((f32[1,262144]{1,0:T(1,128)S(1)}, f32[1,262144]{1,0:T(1,128)S(1)}, u32[]{:S(2)}, u32[]{:S(2)}) %collective-permute-start.3) | collective-permute-done | bytes 1048608 | tf_op jit(solution)/shard_map/ppermute | solution.py:19
  142.1 26.7 %collective-permute-done.4 = f32[1,262144]{1,0:T(1,128)} collective-permute-done((f32[1,262144]{1,0:T(1,128)S(1)}, f32[1,262144]{1,0:T(1,128)}, u32[]{:S(2)}, u32[]{:S(2)}) %collective-permute-start.4) | collective-permute-done | bytes 1048608 | tf_op jit(solution)/shard_map/ppermute | solution.py:19
  169.9 25.3 %collective-permute-done.5 = f32[1,262144]{1,0:T(1,128)} collective-permute-done((f32[1,262144]{1,0:T(1,128)}, f32[1,262144]{1,0:T(1,128)}, u32[]{:S(2)}, u32[]{:S(2)}) %collective-permute-start.5) | collective-permute-done | bytes 1048608 | tf_op jit(solution)/shard_map/ppermute | solution.py:19
  195.2 13.9 %broadcast_multiply_fusion = (f32[2,262144]{1,0:T(2,128)S(1)}, f32[2,262144]{1,0:T(2,128)S(1)}, f32[2,262144]{1,0:T(2,128)}, f32[2,262144]{1,0:T(2,128)}) fusion(f32[2,262144]{1,0:T(2,128)} %all-gather.2.cloned.1.call-done, f32[262144]{0:T(1024)} %bitcast.125, f32[262144]{0:T(1024)} %bitcast.86, f32[262144]{0:T(1024)} %bitcast.343, f32[262144]{0:T(1024)S(1)} %bitcast.341), kind=kLoop, calls=%fused_computation.103 | loop fusion | flops 2097152 | bytes 14680064 | tf_op jit(solution)/shard_map/mul | solution.py:55
  209.1 13.2 %slice_reduce_fusion.1 = (f32[262144]{0:T(1024)}, f32[262144]{0:T(1024)}, f32[262144]{0:T(1024)}, f32[262144]{0:T(1024)}) fusion(f32[2,262144]{1,0:T(2,128)S(1)} %get-tuple-element.21, f32[2,262144]{1,0:T(2,128)S(1)} %get-tuple-element.22), kind=kLoop, calls=%fused_computation.96 | loop fusion | bytes 8388608 | tf_op jit(solution)/shard_map/slice | solution.py:59
  222.4 2.7 stack.90
  225.0 3.4 copy.67
  228.4 2.7 stack.91
  231.1 3.3 copy.68
  234.4 5.9 fusion.105
  240.3 8.7 %fusion.80 = f32[2,64,64,64,1]{3,2,0,1,4:T(8,128)S(1)} fusion(f32[2,64,64,64,1]{3,2,0,1,4:T(8,128)S(1)} %fusion.105, f32[1,64,2,64]{3,1,2,0:T(8,128)S(1)} %get-tuple-element.28, f32[1,64,2,64]{3,1,2,0:T(8,128)S(1)} %get-tuple-element.27), kind=kOutput, calls=%fused_computation.72 | convolution fusion | flops 805322752 | bytes 4259840 | tf_op jit(solution)/shard_map/qmpa,zpabc->zqbcm/dot_general | solution.py:46
  249.0 8.9 %fusion.29 = f32[2,64,64,64,1]{3,2,0,1,4:T(8,128)S(1)} fusion(f32[2,64,64,64,1]{3,2,0,1,4:T(8,128)S(1)} %fusion.80, f32[64,64,64]{2,1,0:T(8,128)S(1)} %add_divide_fusion, f32[1,64,2,64]{3,1,2,0:T(8,128)S(1)} %get-tuple-element.28, f32[1,64,2,64]{3,1,2,0:T(8,128)S(1)} %get-tuple-element.27), kind=kOutput, calls=%fused_computation.35 | convolution fusion | flops 805847040 | bytes 5308416 | tf_op jit(solution)/shard_map/qmpa,zpabc->zqbcm/dot_general | solution.py:46
  258.0 9.1 %fusion.83 = f32[2,64,64,64,1]{3,2,0,1,4:T(8,128)S(1)} fusion(f32[2,64,64,64,1]{3,2,0,1,4:T(8,128)S(1)} %fusion.29, f32[1,64,2,64]{3,1,2,0:T(8,128)S(1)} %get-tuple-element.26, f32[1,64,2,64]{3,1,2,0:T(8,128)S(1)} %get-tuple-element.25), kind=kOutput, calls=%fused_computation.73 | convolution fusion | flops 805322752 | bytes 4259840 | tf_op jit(solution)/shard_map/qmpa,zpabc->zqbcm/dot_general | solution.py:46
  267.1 8.7 %fusion.86 = f32[2,64,64,64,1]{3,2,0,1,4:T(8,128)S(1)} fusion(f32[2,64,64,64,1]{3,2,0,1,4:T(8,128)S(1)} %fusion.83, f32[1,64,2,64]{3,1,2,0:T(8,128)S(1)} %get-tuple-element.26, f32[1,64,2,64]{3,1,2,0:T(8,128)S(1)} %get-tuple-element.25), kind=kOutput, calls=%fused_computation.74 | convolution fusion | flops 805322752 | bytes 4259840 | tf_op jit(solution)/shard_map/qmpa,zpabc->zqbcm/dot_general | solution.py:46
  275.8 8.6 %fusion.89 = f32[1,2,64,64,64]{4,3,1,2,0:T(8,128)S(1)} fusion(f32[2,64,64,64,1]{3,2,0,1,4:T(8,128)S(1)} %fusion.86, f32[1,64,2,64]{3,1,2,0:T(8,128)S(1)} %get-tuple-element.26, f32[1,64,2,64]{3,1,2,0:T(8,128)S(1)} %get-tuple-element.25), kind=kOutput, calls=%fused_computation.75 | convolution fusion | flops 805322752 | bytes 4259840 | tf_op jit(solution)/shard_map/qmpa,zpabc->zqbcm/dot_general | solution.py:46
  284.4 2.4 fusion.135
  286.8 3.9 concatenate.46
  290.6 3.9 concatenate.47
  294.5 2.7 stack.93
  297.2 3.4 copy.74
  300.6 2.7 stack.94
  303.2 3.3 copy.75
  306.6 6.2 %fusion.104 = f32[2,64,64,64,1]{3,2,0,1,4:T(8,128)S(1)} fusion(f32[1,1,64,64,64]{2,4,1,3,0:T(8,128)} %copy.75, f32[1,1,64,64,64]{2,4,1,3,0:T(8,128)} %copy.74, f32[1,64,2,64]{3,1,2,0:T(8,128)S(1)} %get-tuple-element.28, f32[1,64,2,64]{3,1,2,0:T(8,128)S(1)} %get-tuple-element.27), kind=kOutput, calls=%fused_computation.80 | convolution fusion | flops 805847040 | bytes 4259840 | tf_op jit(solution)/shard_map/qmpa,zpabc->zqbcm/dot_general | solution.py:46
  312.7 8.7 %fusion.92 = f32[2,64,64,64,1]{3,2,0,1,4:T(8,128)S(1)} fusion(f32[2,64,64,64,1]{3,2,0,1,4:T(8,128)S(1)} %fusion.104, f32[1,64,2,64]{3,1,2,0:T(8,128)S(1)} %get-tuple-element.28, f32[1,64,2,64]{3,1,2,0:T(8,128)S(1)} %get-tuple-element.27), kind=kOutput, calls=%fused_computation.76 | convolution fusion | flops 805322752 | bytes 4259840 | tf_op jit(solution)/shard_map/qmpa,zpabc->zqbcm/dot_general | solution.py:46
  321.4 8.9 %fusion.18 = f32[2,64,64,64,1]{3,2,0,1,4:T(8,128)S(1)} fusion(f32[2,64,64,64,1]{3,2,0,1,4:T(8,128)S(1)} %fusion.92, f32[64,64,64]{2,1,0:T(8,128)S(1)} %add_divide_fusion, f32[1,64,2,64]{3,1,2,0:T(8,128)S(1)} %get-tuple-element.28, f32[1,64,2,64]{3,1,2,0:T(8,128)S(1)} %get-tuple-element.27), kind=kOutput, calls=%fused_computation.23 | convolution fusion | flops 805847040 | bytes 5308416 | tf_op jit(solution)/shard_map/qmpa,zpabc->zqbcm/dot_general | solution.py:46
  330.3 8.9 %fusion.95 = f32[2,64,64,64,1]{3,2,0,1,4:T(8,128)S(1)} fusion(f32[2,64,64,64,1]{3,2,0,1,4:T(8,128)S(1)} %fusion.18, f32[1,64,2,64]{3,1,2,0:T(8,128)S(1)} %get-tuple-element.26, f32[1,64,2,64]{3,1,2,0:T(8,128)S(1)} %get-tuple-element.25), kind=kOutput, calls=%fused_computation.77 | convolution fusion | flops 805322752 | bytes 4259840 | tf_op jit(solution)/shard_map/qmpa,zpabc->zqbcm/dot_general | solution.py:46
  339.2 8.4 %fusion.98 = f32[2,64,64,64,1]{3,2,0,1,4:T(8,128)S(1)} fusion(f32[2,64,64,64,1]{3,2,0,1,4:T(8,128)S(1)} %fusion.95, f32[1,64,2,64]{3,1,2,0:T(8,128)S(1)} %get-tuple-element.26, f32[1,64,2,64]{3,1,2,0:T(8,128)S(1)} %get-tuple-element.25), kind=kOutput, calls=%fused_computation.78 | convolution fusion | flops 805322752 | bytes 4259840 | tf_op jit(solution)/shard_map/qmpa,zpabc->zqbcm/dot_general | solution.py:46
  347.6 8.7 %fusion.101 = f32[1,2,64,64,64]{4,3,1,2,0:T(8,128)S(1)} fusion(f32[2,64,64,64,1]{3,2,0,1,4:T(8,128)S(1)} %fusion.98, f32[1,64,2,64]{3,1,2,0:T(8,128)S(1)} %get-tuple-element.26, f32[1,64,2,64]{3,1,2,0:T(8,128)S(1)} %get-tuple-element.25), kind=kOutput, calls=%fused_computation.79 | convolution fusion | flops 805322752 | bytes 4259840 | tf_op jit(solution)/shard_map/qmpa,zpabc->zqbcm/dot_general | solution.py:46
  356.4 2.4 fusion.134
  358.8 3.9 concatenate.49
  362.7 3.9 concatenate.50
  366.6 17.0 %slice_reduce_fusion.5 = (f32[262144]{0:T(1024)}, f32[262144]{0:T(1024)}, f32[262144]{0:T(1024)}, f32[262144]{0:T(1024)}) fusion(f32[2,262144]{1,0:T(2,128)} %get-tuple-element.23, f32[2,262144]{1,0:T(2,128)} %get-tuple-element.24), kind=kLoop, calls=%fused_computation.100 | loop fusion | bytes 8388608 | tf_op jit(solution)/shard_map/slice | solution.py:59
  383.6 2.7 stack.87
  386.2 3.4 copy.60
  389.7 2.7 stack.88
  392.3 3.3 copy.61
  395.7 6.0 %fusion.106 = f32[2,64,64,64,1]{3,2,0,1,4:T(8,128)S(1)} fusion(f32[1,1,64,64,64]{2,4,1,3,0:T(8,128)} %copy.61, f32[1,1,64,64,64]{2,4,1,3,0:T(8,128)} %copy.60, f32[1,64,2,64]{3,1,2,0:T(8,128)S(1)} %get-tuple-element.28, f32[1,64,2,64]{3,1,2,0:T(8,128)S(1)} %get-tuple-element.27), kind=kOutput, calls=%fused_computation.82 | convolution fusion | flops 805847040 | bytes 4259840 | tf_op jit(solution)/shard_map/qmpa,zpabc->zqbcm/dot_general | solution.py:46
  401.6 8.7 %fusion.68 = f32[2,64,64,64,1]{3,2,0,1,4:T(8,128)S(1)} fusion(f32[2,64,64,64,1]{3,2,0,1,4:T(8,128)S(1)} %fusion.106, f32[1,64,2,64]{3,1,2,0:T(8,128)S(1)} %get-tuple-element.28, f32[1,64,2,64]{3,1,2,0:T(8,128)S(1)} %get-tuple-element.27), kind=kOutput, calls=%fused_computation.68 | convolution fusion | flops 805322752 | bytes 4259840 | tf_op jit(solution)/shard_map/qmpa,zpabc->zqbcm/dot_general | solution.py:46
  410.3 9.1 %fusion.40 = f32[2,64,64,64,1]{3,2,0,1,4:T(8,128)S(1)} fusion(f32[2,64,64,64,1]{3,2,0,1,4:T(8,128)S(1)} %fusion.68, f32[64,64,64]{2,1,0:T(8,128)S(1)} %add_divide_fusion, f32[1,64,2,64]{3,1,2,0:T(8,128)S(1)} %get-tuple-element.28, f32[1,64,2,64]{3,1,2,0:T(8,128)S(1)} %get-tuple-element.27), kind=kOutput, calls=%fused_computation.47 | convolution fusion | flops 805847040 | bytes 5308416 | tf_op jit(solution)/shard_map/qmpa,zpabc->zqbcm/dot_general | solution.py:46
  419.5 8.9 %fusion.71 = f32[2,64,64,64,1]{3,2,0,1,4:T(8,128)S(1)} fusion(f32[2,64,64,64,1]{3,2,0,1,4:T(8,128)S(1)} %fusion.40, f32[1,64,2,64]{3,1,2,0:T(8,128)S(1)} %get-tuple-element.26, f32[1,64,2,64]{3,1,2,0:T(8,128)S(1)} %get-tuple-element.25), kind=kOutput, calls=%fused_computation.69 | convolution fusion | flops 805322752 | bytes 4259840 | tf_op jit(solution)/shard_map/qmpa,zpabc->zqbcm/dot_general | solution.py:46
  428.3 8.4 %fusion.74 = f32[2,64,64,64,1]{3,2,0,1,4:T(8,128)S(1)} fusion(f32[2,64,64,64,1]{3,2,0,1,4:T(8,128)S(1)} %fusion.71, f32[1,64,2,64]{3,1,2,0:T(8,128)S(1)} %get-tuple-element.26, f32[1,64,2,64]{3,1,2,0:T(8,128)S(1)} %get-tuple-element.25), kind=kOutput, calls=%fused_computation.70 | convolution fusion | flops 805322752 | bytes 4259840 | tf_op jit(solution)/shard_map/qmpa,zpabc->zqbcm/dot_general | solution.py:46
  436.7 8.7 %fusion.77 = f32[1,2,64,64,64]{4,3,1,2,0:T(8,128)S(1)} fusion(f32[2,64,64,64,1]{3,2,0,1,4:T(8,128)S(1)} %fusion.74, f32[1,64,2,64]{3,1,2,0:T(8,128)S(1)} %get-tuple-element.26, f32[1,64,2,64]{3,1,2,0:T(8,128)S(1)} %get-tuple-element.25), kind=kOutput, calls=%fused_computation.71 | convolution fusion | flops 805322752 | bytes 4259840 | tf_op jit(solution)/shard_map/qmpa,zpabc->zqbcm/dot_general | solution.py:46
  445.5 2.2 fusion.136
  447.7 3.9 concatenate.43
  451.6 4.0 concatenate.44
  455.6 2.7 stack.74
  458.2 3.3 copy.53
  461.5 2.7 stack.75
  464.3 3.3 copy.54
  467.6 5.9 fusion.107
  473.5 8.7 %fusion.56 = f32[2,64,64,64,1]{3,2,0,1,4:T(8,128)S(1)} fusion(f32[2,64,64,64,1]{3,2,0,1,4:T(8,128)S(1)} %fusion.107, f32[1,64,2,64]{3,1,2,0:T(8,128)S(1)} %get-tuple-element.28, f32[1,64,2,64]{3,1,2,0:T(8,128)S(1)} %get-tuple-element.27), kind=kOutput, calls=%fused_computation.64 | convolution fusion | flops 805322752 | bytes 4259840 | tf_op jit(solution)/shard_map/qmpa,zpabc->zqbcm/dot_general | solution.py:46
  482.2 8.9 %fusion.51 = f32[2,64,64,64,1]{3,2,0,1,4:T(8,128)S(1)} fusion(f32[2,64,64,64,1]{3,2,0,1,4:T(8,128)S(1)} %fusion.56, f32[64,64,64]{2,1,0:T(8,128)S(1)} %add_divide_fusion, f32[1,64,2,64]{3,1,2,0:T(8,128)S(1)} %get-tuple-element.28, f32[1,64,2,64]{3,1,2,0:T(8,128)S(1)} %get-tuple-element.27), kind=kOutput, calls=%fused_computation.59 | convolution fusion | flops 805847040 | bytes 5308416 | tf_op jit(solution)/shard_map/qmpa,zpabc->zqbcm/dot_general | solution.py:46
  491.2 9.1 %fusion.59 = f32[2,64,64,64,1]{3,2,0,1,4:T(8,128)S(1)} fusion(f32[2,64,64,64,1]{3,2,0,1,4:T(8,128)S(1)} %fusion.51, f32[1,64,2,64]{3,1,2,0:T(8,128)S(1)} %get-tuple-element.26, f32[1,64,2,64]{3,1,2,0:T(8,128)S(1)} %get-tuple-element.25), kind=kOutput, calls=%fused_computation.65 | convolution fusion | flops 805322752 | bytes 4259840 | tf_op jit(solution)/shard_map/qmpa,zpabc->zqbcm/dot_general | solution.py:46
  500.3 8.7 %fusion.62 = f32[2,64,64,64,1]{3,2,0,1,4:T(8,128)S(1)} fusion(f32[2,64,64,64,1]{3,2,0,1,4:T(8,128)S(1)} %fusion.59, f32[1,64,2,64]{3,1,2,0:T(8,128)S(1)} %get-tuple-element.26, f32[1,64,2,64]{3,1,2,0:T(8,128)S(1)} %get-tuple-element.25), kind=kOutput, calls=%fused_computation.66 | convolution fusion | flops 805322752 | bytes 4259840 | tf_op jit(solution)/shard_map/qmpa,zpabc->zqbcm/dot_general | solution.py:46
  509.0 8.6 %fusion.65 = f32[1,2,64,64,64]{4,3,1,2,0:T(8,128)S(1)} fusion(f32[2,64,64,64,1]{3,2,0,1,4:T(8,128)S(1)} %fusion.62, f32[1,64,2,64]{3,1,2,0:T(8,128)S(1)} %get-tuple-element.26, f32[1,64,2,64]{3,1,2,0:T(8,128)S(1)} %get-tuple-element.25), kind=kOutput, calls=%fused_computation.67 | convolution fusion | flops 805322752 | bytes 4259840 | tf_op jit(solution)/shard_map/qmpa,zpabc->zqbcm/dot_general | solution.py:46
  519.4 3.9 concatenate.40
  523.2 2.3 concatenate.41
  525.6 13.9 %fusion.118 = f32[2,262144]{1,0:T(2,128)} fusion(f32[1,262144]{1,0:T(1,128)} %concatenate.41, f32[1,262144]{1,0:T(1,128)} %concatenate.40, f32[1,262144]{1,0:T(1,128)} %concatenate.44, f32[1,262144]{1,0:T(1,128)} %concatenate.43, f32[1,262144]{1,0:T(1,128)} %concatenate.47, f32[1,262144]{1,0:T(1,128)} %concatenate.46, f32[1,262144]{1,0:T(1,128)} %concatenate.50, ...), kind=kLoop, calls=%fused_computation.87 | loop fusion | flops 5767168 | bytes 14680064 | tf_op jit(solution)/shard_map/add | solution.py:82
  540.8 47.2 %all-reduce.3.cloned.1.call-done = f32[2,262144]{1,0:T(2,128)} async-done(((f32[2,262144]{1,0:T(2,128)}), f32[2,262144]{1,0:T(2,128)}) %all-reduce.3.cloned.1.call-update) | async-done | bytes 2097168
  (30 shorter events, 11.3 us)
Async XLA Ops:
  6.5 163.4 %all-gather.2.cloned.1.call-start = ((), (), s32[]{:S(2)}) async-start(), calls=%async_computation | async-start | bytes 2621440 | tf_op jit(solution)/shard_map/all_gather | solution.py:67
  9.0 29.2 %collective-permute-start = (f32[1,262144]{1,0:T(1,128)S(1)}, f32[1,262144]{1,0:T(1,128)S(1)}, u32[]{:S(2)}, u32[]{:S(2)}) collective-permute-start(f32[1,262144]{1,0:T(1,128)S(1)} %broadcast_multiply_fusion.4), channel_id=1, source_target_pairs={{7,0},{0,1},{1,2},{2,3},{3,4},{4,5},{5,6},{6,7},{15,8},{8,9},{9,10... | collective-permute-start | bytes 3145736 | tf_op jit(solution)/shard_map/ppermute | solution.py:19
  40.4 26.2 %collective-permute-start.1 = (f32[1,262144]{1,0:T(1,128)S(1)}, f32[1,262144]{1,0:T(1,128)S(1)}, u32[]{:S(2)}, u32[]{:S(2)}) collective-permute-start(f32[1,262144]{1,0:T(1,128)S(1)} %broadcast_select_fusion), channel_id=1, source_target_pairs={{6,0},{7,1},{0,2},{1,3},{2,4},{3,5},{4,6},{5,7},{14,8},{15,9},{8,1... | collective-permute-start | bytes 3145736 | tf_op jit(solution)/shard_map/ppermute | solution.py:19
  67.7 45.1 %collective-permute-start.2 = (f32[1,262144]{1,0:T(1,128)S(1)}, f32[1,262144]{1,0:T(1,128)S(1)}, u32[]{:S(2)}, u32[]{:S(2)}) collective-permute-start(f32[1,262144]{1,0:T(1,128)S(1)} %broadcast_select_fusion.1), channel_id=1, source_target_pairs={{4,0},{5,1},{6,2},{7,3},{0,4},{1,5},{2,6},{3,7},{12,8},{13,9},{14,... | collective-permute-start | bytes 3145736 | tf_op jit(solution)/shard_map/ppermute | solution.py:19
  114.0 27.8 %collective-permute-start.3 = (f32[1,262144]{1,0:T(1,128)S(1)}, f32[1,262144]{1,0:T(1,128)S(1)}, u32[]{:S(2)}, u32[]{:S(2)}) collective-permute-start(f32[1,262144]{1,0:T(1,128)S(1)} %broadcast_select_fusion.2), channel_id=1, source_target_pairs={{7,0},{0,1},{1,2},{2,3},{3,4},{4,5},{5,6},{6,7},{15,8},{8,9},{9,10... | collective-permute-start | bytes 3145736 | tf_op jit(solution)/shard_map/ppermute | solution.py:19
  114.0 474.0 %all-reduce.3.cloned.1.call-start = ((), (), s32[]{:S(2)}) async-start(), calls=%async_computation.1 | async-start | bytes 4194304
  141.8 27.3 %copy-start = (f32[1,262144]{1,0:T(1,128)}, f32[1,262144]{1,0:T(1,128)S(1)}, u32[]{:S(2)}) copy-start(f32[1,262144]{1,0:T(1,128)S(1)} %collective-permute-done.3) | copy-start | bytes 3145732
  141.8 27.0 %collective-permute-start.4 = (f32[1,262144]{1,0:T(1,128)S(1)}, f32[1,262144]{1,0:T(1,128)}, u32[]{:S(2)}, u32[]{:S(2)}) collective-permute-start(f32[1,262144]{1,0:T(1,128)S(1)} %collective-permute-done.3), channel_id=1, source_target_pairs={{7,0},{0,1},{1,2},{2,3},{3,4},{4,5},{5,6},{6,7},{15,8},{8,9},{9,10... | collective-permute-start | bytes 3145736 | tf_op jit(solution)/shard_map/ppermute | solution.py:19
  168.8 26.4 %collective-permute-start.5 = (f32[1,262144]{1,0:T(1,128)}, f32[1,262144]{1,0:T(1,128)}, u32[]{:S(2)}, u32[]{:S(2)}) collective-permute-start(f32[1,262144]{1,0:T(1,128)} %collective-permute-done.4), channel_id=1, source_target_pairs={{7,0},{0,1},{1,2},{2,3},{3,4},{4,5},{5,6},{6,7},{15,8},{8,9},{9,10... | collective-permute-start | bytes 3145736 | tf_op jit(solution)/shard_map/ppermute | solution.py:19
  525.6 14.0 %copy-start.1 = (u32[32]{0:T(128)S(1)}, u32[32]{0:T(128)}, u32[]{:S(2)}) copy-start(u32[32]{0:T(128)} %constant.113) | copy-start | bytes 388
Sparse Core Ops, SparseCore 0:
  114.2 23.6 all-gather.1
  539.7 48.2 all-reduce.2
where the time goes:
time: 602 us; the launch traced here: 597 us
  waiting for transfers between devices  220 us (37%)
  matrix products  199 us (33%)
  local copies, waits for them, and re-layouts  119 us (20%)
  other arithmetic  37.4 us (6%)
  between operations  18.1 us (3%)
    dot_general x24, matrix products, transform(): jnp.einsum('qmpa,zpabc->zqbcm', dft_matrix, grid_field, precision=lax.Pre...  199 us
    ppermute x6, waiting for transfers between devices, shifted(): return lax.ppermute(block, axis, route)  173 us
    another operation x16, local copies, waits for them, and re-layouts, exchange_terms(): packed = jnp.stack([density[:half_count], density[half_count:]], axis=1)  48.2 us
    unnamed x3, waiting for transfers between devices  47.2 us
    slice x2, local copies, waits for them, and re-layouts, exchange_terms(): packed = jnp.stack([density[:half_count], density[half_count:]], axis=1)  30.2 us
    concatenate x8, local copies, waits for them, and re-layouts, exchange_terms(): potential = jnp.concatenate([both_parts[:, 0], both_parts[:, 1]], axis=0)  29.6 us
    add x1, other arithmetic, local(): accumulated + exchange_terms(whole_targets, visiting, kernel_grid, forwar...  13.9 us
    mul x1, other arithmetic, exchange_terms(): target_rows[:, None, :] * source_rows[None, :, :]  13.9 us
  transfers between devices with their start and end apart: 8, of which 7 were waited for; matrix products, arithmetic and copies ran while one was open for 1% of the time, Pallas kernels for 0%

commit v1 on v0

v1 whole, which is shorter than its diff:
```python
import functools
import math

import jax
import jax.numpy as jnp
import numpy as np
from jax import lax
from jax.experimental import pallas as pl
from jax.experimental.pallas import tpu as pltpu
from jax.sharding import PartitionSpec as P

NG = 64
STOPS = 4
LANES = 128

box_length = 16.0
screen_square = 0.25


def split_np(table):
    high = table.astype(jnp.bfloat16)
    low = (table - high.astype(np.float64)).astype(jnp.bfloat16)
    return high, low


def stacked(table):
    high, low = split_np(table)
    return np.concatenate(
        [np.concatenate([high, high], axis=1), np.concatenate([low, low], axis=1)], axis=0
    )


def tables():
    counter = np.arange(NG)
    angle = 2.0 * np.pi * (counter[:, None] * counter[None, :] % NG) / NG
    cas = (np.cos(angle) + np.sin(angle)) / math.sqrt(NG)
    order = np.concatenate([counter[0::2], counter[1::2]])
    along_x = stacked(cas)
    along_y = stacked(cas[:, order])
    back_y = stacked(cas[order, :])
    blocks = np.kron(np.eye(4), cas)
    z_high, z_low = split_np(blocks)
    freq = np.where(counter < NG // 2, counter, counter - NG)
    wave = (2.0 * np.pi * freq / box_length) ** 2
    plane = wave[:, None] + np.tile(wave, 2)[None, :] + screen_square
    return along_x, along_y, back_y, z_high, z_low, plane.astype(np.float32), wave.astype(np.float32)


def split(value):
    high = value.astype(jnp.bfloat16)
    low = (value - high.astype(jnp.float32)).astype(jnp.bfloat16)
    return high, low


def left(table, value):
    high, low = split(value)
    both = jnp.dot(
        table, jnp.concatenate([high, low], axis=0), preferred_element_type=jnp.float32
    )
    return both[:NG] + both[NG:]


def right(z_high, z_low, value):
    high, low = split(value)
    dot = functools.partial(jnp.dot, preferred_element_type=jnp.float32)
    return dot(high, z_high) + (dot(low, z_high) + dot(high, z_low))


HALF = NG // 2
XB = 4


def pair_kernel(count, has_prior, slots, wave, *refs):
    pool = refs[:count]
    refs = refs[count:]
    targets, along_x, along_y, back_y, z_high, z_low, plane = refs[:7]
    refs = refs[7:]
    if has_prior:
        prior, refs = refs[0], refs[1:]
    out, src, field, sems = refs

    for s in range(2):
        for i in range(count):
            @pl.when(slots[s] == i)
            def _():
                pltpu.make_async_copy(pool[i], src.at[s], sems.at[s]).start()
    for s in range(2):
        pltpu.make_async_copy(pool[0], src.at[s], sems.at[s]).wait()

    first = lax.broadcasted_iota(jnp.int32, (HALF, LANES), 1) < NG

    def interleave(a, b):
        even = jnp.where(first, a, pltpu.roll(b, NG, 1))
        odd = jnp.where(first, pltpu.roll(a, NG, 1), b)
        return even, odd

    def source_rows(s, x):
        v = src[s, pl.ds(pl.multiple_of(x * HALF, HALF), HALF), :]
        even, odd = interleave(v, v)
        return jnp.concatenate([even, odd], axis=0)

    def source_plane(x):
        return jnp.concatenate([source_rows(0, x), source_rows(1, x)], axis=1)

    def forward(step, carry):
        slabs = []
        for k in range(XB):
            x = step * XB + k
            rows = pl.ds(pl.multiple_of(x * HALF, HALF), HALF)
            even, odd = interleave(targets[0, rows, :], targets[1, rows, :])
            t = jnp.concatenate([even, odd], axis=0)
            slabs.append(jnp.concatenate([t, t], axis=1) * source_plane(x))
        lines = right(z_high[...], z_low[...], jnp.concatenate(slabs, axis=0))
        for k in range(XB):
            x = step * XB + k
            r = left(along_y[...], lines[k * NG : (k + 1) * NG])
            rows = pl.ds(pl.multiple_of(x * NG, NG), NG)
            field[0, rows, :] = r[:, :LANES]
            field[1, rows, :] = r[:, LANES:]
        return carry

    def middle(y, carry):
        rows = pl.ds(y, NG, stride=NG)
        v = jnp.concatenate([field[0, rows, :], field[1, rows, :]], axis=1)
        v = left(along_x[...], v)
        factor = (4.0 * math.pi) / (plane[...] + wave[y])
        v = left(along_x[...], v * jnp.concatenate([factor, factor], axis=1))
        field[0, rows, :] = v[:, :LANES]
        field[1, rows, :] = v[:, LANES:]
        return carry

    def backward(step, carry):
        slabs = []
        for k in range(XB):
            x = step * XB + k
            rows = pl.ds(pl.multiple_of(x * NG, NG), NG)
            v = jnp.concatenate([field[0, rows, :], field[1, rows, :]], axis=1)
            slabs.append(left(back_y[...], v))
        lines = right(z_high[...], z_low[...], jnp.concatenate(slabs, axis=0))
        for k in range(XB):
            x = step * XB + k
            v = lines[k * NG : (k + 1) * NG] * source_plane(x)
            v = v[:, :LANES] + v[:, LANES:]
            a, b = interleave(v[:HALF], v[HALF:])
            rows = pl.ds(pl.multiple_of(x * HALF, HALF), HALF)
            if has_prior:
                out[0, rows, :] = prior[0, rows, :] - a
                out[1, rows, :] = prior[1, rows, :] - b
            else:
                out[0, rows, :] = -a
                out[1, rows, :] = -b
        return carry

    lax.fori_loop(0, NG // XB, forward, 0)
    lax.fori_loop(0, NG, middle, 0, unroll=2)
    lax.fori_loop(0, NG // XB, backward, 0)


def exchange_terms(slots, pool, targets, prior, consts):
    *mats, wave = consts
    rows = targets.shape[1]
    smem = pl.BlockSpec(memory_space=pltpu.SMEM)
    vmem = pl.BlockSpec(memory_space=pltpu.VMEM)
    anywhere = pl.BlockSpec(memory_space=pl.ANY)
    extra = [] if prior is None else [prior]
    return pl.pallas_call(
        functools.partial(pair_kernel, len(pool), prior is not None),
        out_shape=jax.ShapeDtypeStruct(targets.shape, jnp.float32),
        in_specs=[smem, smem] + [anywhere] * len(pool) + [vmem] * (1 + len(mats) + len(extra)),
        out_specs=vmem,
        scratch_shapes=[
            pltpu.VMEM((2, rows, LANES), jnp.float32),
            pltpu.VMEM((2, NG * NG, LANES), jnp.float32),
            pltpu.SemaphoreType.DMA((2,)),
        ],
        compiler_params=pltpu.CompilerParams(vmem_limit_bytes=40 * 1024 * 1024),
        cost_estimate=pl.CostEstimate(
            flops=20_000_000_000, bytes_accessed=8_000_000, transcendentals=0
        ),
    )(slots, wave, *pool, targets, *mats, *extra)


def ring_order(count):
    return list(range(0, count, 2)) + list(range(1, count, 2))[::-1]


def arrival(count):
    order = ring_order(count)
    place = [order.index(i) for i in range(count)]
    worst = [0] * STOPS
    for b in range(count):
        for off in range(count):
            steps = []
            for k in range(STOPS):
                d = (place[b] - place[(b - off - k) % count]) % count
                steps.append(min(d, count - d))
            worst = [max(w, s) for w, s in zip(worst, sorted(steps))]
    return worst[1], worst[3]


def partner(value, axis, bit):
    return lax.ppermute(value, axis, [(i, i ^ bit) for i in range(lax.axis_size(axis))])


def gather_rows(quarter, axis):
    me = lax.axis_index(axis)
    count = lax.axis_size(axis)
    parts = {0: quarter}
    bit = count // 2
    while bit:
        for key, value in list(parts.items()):
            parts[key ^ bit] = partner(value, axis, bit)
        bit //= 2
    ordered = []
    keys = sorted(parts)
    level = [parts[k] for k in keys]
    bit = 1
    while bit < count:
        swap = (me // bit) % 2 == 1
        merged = []
        for i in range(0, len(level), 2):
            a, b = level[i], level[i + 1]
            merged.append(
                jnp.concatenate([jnp.where(swap, b, a), jnp.where(swap, a, b)], axis=1)
            )
        level = merged
        bit *= 2
    return level[0]


def scatter_rows(total, axis):
    me = lax.axis_index(axis)
    count = lax.axis_size(axis)
    targets, rows, lanes = total.shape
    value = total.reshape((targets, count, rows // count, lanes))
    bit = 1
    while bit < count:
        mine = (me // bit) % 2 == 1
        pairs = value.reshape((targets, value.shape[1] // 2, 2) + value.shape[2:])
        low, high = pairs[:, :, 0], pairs[:, :, 1]
        value = jnp.where(mine, high, low) + partner(jnp.where(mine, low, high), axis, bit)
        bit *= 2
    return value[:, 0]


def local(targets, sources, occupation, offsets):
    count = lax.axis_size("blk")
    target_count, cells = targets.shape[0], sources.shape[1]
    consts = [jnp.asarray(v) for v in tables()]
    scaled = sources * jnp.sqrt(occupation.astype(jnp.float32) * 0.5)[:, None]
    scaled = scaled.reshape(cells // LANES, LANES)
    quarter = targets.reshape(target_count, targets.shape[1] // LANES, LANES)
    whole = gather_rows(quarter, "grp")

    order = ring_order(count)
    up = [(order[i], order[(i + 1) % count]) for i in range(count)]
    down = [(b, a) for a, b in up]
    first_step, last_step = arrival(count)
    pool = [scaled]
    ahead = behind = scaled
    for step in range(1, count // 2 + 1):
        if step < count // 2:
            ahead = lax.ppermute(ahead, "blk", up)
            behind = lax.ppermute(behind, "blk", down)
            pool += [ahead, behind]
        else:
            half = scaled.shape[0] // 2
            upper = lax.ppermute(ahead[:half], "blk", up)
            lower = lax.ppermute(behind[half:], "blk", down)
            pool += [jnp.concatenate([upper, lower], axis=0)]

    place = np.zeros(count, np.int32)
    place[order] = np.arange(count)
    place = jnp.asarray(place)
    me = lax.axis_index("blk")
    offset = lax.dynamic_index_in_dim(offsets, lax.axis_index("grp"), 0, keepdims=False)
    block = (me - offset - jnp.arange(STOPS, dtype=jnp.int32)) % count
    back = (place[me] - place[block]) % count
    slot = jnp.where(
        back == 0, 0, jnp.where(back <= count // 2, 2 * back - 1, 2 * (count - back))
    ).astype(jnp.int32)
    rank = jnp.sum((slot[None, :] < slot[:, None]).astype(jnp.int32), axis=1)
    ranked = jnp.sum(
        jnp.where(rank[None, :] == jnp.arange(STOPS)[:, None], slot[None, :], 0), axis=1
    ).astype(jnp.int32)

    early = pool[: 2 * first_step + 1]
    late = pool[: 2 * last_step + 1]
    partial = exchange_terms(ranked[:2], early, whole, None, consts)
    total = exchange_terms(ranked[2:], late, whole, partial, consts)
    return scatter_rows(total, "grp").reshape(targets.shape)


def solution(mesh):
    in_specs = (P("blk", "grp"), P(("grp", "blk"), None), P(("grp", "blk")), P())
    out_specs = P("blk", "grp")
    return jax.shard_map(local, mesh=mesh, in_specs=in_specs, out_specs=out_specs, check_vma=False)
```

time: 602 us -> 172 us (0.29)
  matrix products: 199 us -> 0 us
  waiting for transfers between devices: 220 us -> 72.8 us
  local copies, waits for them, and re-layouts: 119 us -> 6.25 us
  Pallas kernels: 0 us -> 71.9 us
  other arithmetic: 37.4 us -> 6.13 us
  between operations: 18.1 us -> 1.61 us
  starting transfers between devices: 3.28 us -> 12.3 us
    dot_general x24 -> x0, matrix products: 199 us -> none  [transform(): jnp.einsum('qmpa,zpabc->zqbcm', dft_matrix, grid_field, precision=lax.Pre...]
    ppermute x6 -> x13, waiting for transfers between devices: 173 us -> 72.8 us  [the longest x3 47.5 us: local(): behind = lax.ppermute(behind, 'blk', down)]
    pallas_call x0 -> x2, Pallas kernels: none -> 71.9 us  [exchange_terms(): pl.pallas_call(functools.partial(pair_kernel, len(pool), prior is not Non...]
    another operation x16 -> x0, local copies, waits for them, and re-layouts: 48.2 us -> none  [exchange_terms(): packed = jnp.stack([density[:half_count], density[half_count:]], axis=1)]
    unnamed x3 -> x0, waiting for transfers between devices: 47.2 us -> none
    slice x6 -> x3, local copies, waits for them, and re-layouts: 39 us -> 0.14 us  [the longest x1 0.07 us: local(): partial = exchange_terms(ranked[:2], early, whole, None, consts)]
    concatenate x8 -> x0, local copies, waits for them, and re-layouts: 29.6 us -> none  [exchange_terms(): potential = jnp.concatenate([both_parts[:, 0], both_parts[:, 1]], axis=0)]
    mul x5 -> x0, other arithmetic: 14.4 us -> none  [the longest x1 13.9 us: exchange_terms(): target_rows[:, None, :] * source_rows[None, :, :]]
  transfers between devices with their start and end apart: 8 -> 13, of which waited for: 7 -> 6; matrix products, arithmetic and copies ran while one was open for 1% -> 4% of each run, Pallas kernels for 0% -> 21%
where the time goes in v1:
time: 172 us; the launch traced here: 171 us
  waiting for transfers between devices  72.8 us (42%)
  Pallas kernels  71.9 us (42%)
  starting transfers between devices  12.3 us (7%)
  local copies, waits for them, and re-layouts  6.25 us (4%)
  other arithmetic  6.13 us (4%)
    pallas_call x2, Pallas kernels, exchange_terms(): pl.pallas_call(functools.partial(pair_kernel, len(pool), prior is not Non...  71.9 us
    ppermute x3, waiting for transfers between devices, local(): behind = lax.ppermute(behind, 'blk', down)  47.5 us
    ppermute x5, waiting for transfers between devices, partner(): lax.ppermute(value, axis, [(i, i ^ bit) for i in range(lax.axis_size(axis...  25.3 us
    ppermute x3, starting transfers between devices, local(): behind = lax.ppermute(behind, 'blk', down)  6.13 us
    unnamed x32, local copies, waits for them, and re-layouts  4.28 us
  transfers between devices with their start and end apart: 13, of which 6 were waited for; matrix products, arithmetic and copies ran while one was open for 4% of the time, Pallas kernels for 21%

profile of v1, /device:TPU:0, one launch (start us, length us, event | category | flops | bytes accessed | tf_op | source)
XLA Modules:
  0.0 171.0 jit_solution(5167071774481722065)
XLA Ops:
  0.8 1.8 %broadcast_multiply_fusion = f32[1,262144]{1,0:T(1,128)S(1)} fusion(f32[1,262144]{1,0:T(1,128)} %param.13, f32[]{:T(128)} %bitcast.3), kind=kLoop, calls=%fused_computation.19 | loop fusion | flops 262144 | bytes 2097156 | tf_op jit(solution)/shard_map/mul | solution.py:250
  2.6 3.0 %collective-permute-start.1 = (f32[2048,128]{1,0:T(8,128)S(1)}, f32[2048,128]{1,0:T(8,128)S(1)}, u32[]{:S(2)}, u32[]{:S(2)}) collective-permute-start(f32[2048,128]{1,0:T(8,128)S(1)} %bitcast.70), channel_id=1, source_target_pairs={{2,0},{4,2},{6,4},{7,6},{5,7},{3,5},{1,3},{0,1},{10,8},{12,10},{14... | collective-permute-start | bytes 3145736 | tf_op jit(solution)/shard_map/ppermute | solution.py:264
  5.6 0.1 collective-permute-start
  5.7 23.1 %collective-permute-done.1.refs_2_ = f32[2048,128]{1,0:T(8,128)S(1)} collective-permute-done((f32[2048,128]{1,0:T(8,128)S(1)}, f32[2048,128]{1,0:T(8,128)S(1)}, u32[]{:S(2)}, u32[]{:S(2)}) %collective-permute-start.1) | collective-permute-done | bytes 1048608 | tf_op jit(solution)/shard_map/ppermute | solution.py:264
  28.8 1.7 collective-permute-start.3
  30.5 0.0 collective-permute-done.refs_1_
  30.5 0.3 collective-permute-start.2
  30.9 1.0 copy-done.2
  31.8 0.8 copy.48
  32.7 0.0 collective-permute-start.10
  32.7 1.7 collective-permute-start.8
  34.3 0.0 copy-done.14
  34.3 0.6 dynamic_slice.8
  35.5 0.0 copy-done.12
  35.5 0.6 dynamic_slice.7
  36.1 0.6 gather_fusion
  36.8 0.6 compare_select_fusion.6
  37.4 0.2 convert_reduce_fusion
  37.5 9.8 %collective-permute-done.8 = f32[2,512,128]{2,1,0:T(8,128)} collective-permute-done((f32[2,512,128]{2,1,0:T(8,128)}, f32[2,512,128]{2,1,0:T(8,128)}, u32[]{:S(2)}, u32[]{:S(2)}) %collective-permute-start.8) | collective-permute-done | bytes 524320 | tf_op jit(solution)/shard_map/ppermute | solution.py:202
  47.3 0.0 collective-permute-start.9
  47.3 0.1 select_reduce_fusion
  47.4 5.8 %collective-permute-done.3.refs_4_ = f32[2048,128]{1,0:T(8,128)} collective-permute-done((f32[2048,128]{1,0:T(8,128)S(1)}, f32[2048,128]{1,0:T(8,128)}, u32[]{:S(2)}, u32[]{:S(2)}) %collective-permute-start.3) | collective-permute-done | bytes 1048608 | tf_op jit(solution)/shard_map/ppermute | solution.py:264
  53.3 1.4 collective-permute-start.5
  54.7 0.0 collective-permute-done.2.refs_3_
  54.7 0.6 collective-permute-start.4
  55.3 0.1 fusion.11
  55.4 0.0 collective-permute-done.10
  55.4 1.3 broadcast_select_fusion.1
  56.6 0.0 collective-permute-done.9
  56.7 1.3 broadcast_select_fusion.3
  57.9 0.1 fusion.4
  58.1 0.0 copy-start.4
  58.1 0.0 copy-start.5
  58.1 0.0 copy-start.6
  58.1 0.0 copy-start.7
  58.1 0.0 copy-start.8
  58.1 0.0 copy-start.9
  58.2 0.1 pad_maximum_fusion.refs_7_.refs_8_
  58.3 0.0 copy-start.1
  58.3 0.0 copy-start.3
  58.3 0.0 copy-start.10
  58.3 18.6 %collective-permute-done.5.refs_6_ = f32[2048,128]{1,0:T(8,128)S(1)} collective-permute-done((f32[2048,128]{1,0:T(8,128)}, f32[2048,128]{1,0:T(8,128)S(1)}, u32[]{:S(2)}, u32[]{:S(2)}) %collective-permute-start.5) | collective-permute-done | bytes 1048608 | tf_op jit(solution)/shard_map/ppermute | solution.py:264
  77.0 1.2 collective-permute-start.7
  78.2 0.0 collective-permute-done.4.refs_5_
  78.2 0.9 collective-permute-start.6
  79.2 0.0 copy-done.7
  79.2 0.0 copy-done.8
  79.2 0.0 copy-done.9
  79.2 0.0 copy-done.1
  79.2 35.4 %shard_map.118.refs_15_ = f32[2,2048,128]{2,1,0:T(8,128)S(1)} custom-call(s32[2]{0:T(128)S(1)} %get-tuple-element.11.slots, f32[64]{0:T(128)S(1)} %copy-done.10, f32[2048,128]{1,0:T(8,128)S(1)} %bitcast.72, f32[2048,128]{1,0:T(8,128)S(1)} %copy-done.3, f32[2048,128]{1,0:T(8,128)S(1)} %copy-done.1, f32[2048,128]{1,0:T(8,128)} %collective-permute-done.2.refs_3_, ...), custom_call_target="tpu_custom_call" | custom-call | flops 20000000000 | bytes 8000000 | tf_op jit(solution)/shard_map/pallas_call | solution.py:166
  114.7 0.0 collective-permute-done.7
  114.7 0.0 collective-permute-done.6
  114.7 0.1 pad_maximum_fusion.1.refs_7_
  114.8 1.2 copy-done.11
  116.0 36.5 %shard_map.119 = f32[2,2048,128]{2,1,0:T(8,128)S(1)} custom-call(s32[2]{0:T(128)S(1)} %get-tuple-element.12.slots, f32[64]{0:T(128)S(1)} %copy-done.10, f32[2048,128]{1,0:T(8,128)S(1)} %bitcast.73, f32[2048,128]{1,0:T(8,128)S(1)} %copy-done.3, f32[2048,128]{1,0:T(8,128)S(1)} %copy-done.1, f32[2048,128]{1,0:T(8,128)} %collective-permute-done.2.refs_3_, ...), custom_call_target="tpu_custom_call" | custom-call | flops 20000000000 | bytes 8000000 | tf_op jit(solution)/shard_map/pallas_call | solution.py:166
  152.5 0.1 select_bitcast_fusion
  152.6 0.1 collective-permute-start.11
  152.7 2.6 %collective-permute-done.11 = f32[2,2,512,128]{3,2,1,0:T(8,128)S(1)} collective-permute-done((f32[2,2,512,128]{3,2,1,0:T(8,128)S(1)}, f32[2,2,512,128]{3,2,1,0:T(8,128)S(1)}, u32[]{:S(2)}, u32[]{:S(2)}) %collective-permute-start.11) | collective-permute-done | bytes 1048608 | tf_op jit(solution)/shard_map/ppermute | solution.py:202
  155.3 0.2 fusion.2
  155.6 0.1 select_bitcast_fusion.1
  155.6 1.2 collective-permute-start.12
  156.8 12.8 %collective-permute-done.12 = f32[2,1,512,128]{3,2,0,1:T(8,128)S(1)} collective-permute-done((f32[2,1,512,128]{3,2,0,1:T(8,128)S(1)}, f32[2,1,512,128]{3,2,0,1:T(8,128)S(1)}, u32[]{:S(2)}, u32[]{:S(2)}) %collective-permute-start.12) | collective-permute-done | bytes 524320 | tf_op jit(solution)/shard_map/ppermute | solution.py:202
  169.7 0.1 fusion.7
  169.8 1.2 copy.47
  (17 shorter events, 0.1 us)
Async XLA Ops:
  0.0 35.5 %copy-start.12 = (s32[8]{0:T(128)S(1)}, s32[8]{0:T(128)}, u32[]{:S(2)}) copy-start(s32[8]{0:T(128)} %constant.111.clone) | copy-start | bytes 100
  0.0 31.8 %copy-start.13 = (f32[2,65536]{1,0:T(2,128)S(1)}, f32[2,65536]{1,0:T(2,128)}, u32[]{:S(2)}) copy-start(f32[2,65536]{1,0:T(2,128)} %param.12) | copy-start | bytes 1572868
  0.0 34.3 %copy-start.14 = (s32[4]{0:T(128)S(1)}, s32[4]{0:T(128)}, u32[]{:S(2)}) copy-start(s32[4]{0:T(128)} %param.15) | copy-start | bytes 52
  2.6 26.3 %collective-permute-start.1 = (f32[2048,128]{1,0:T(8,128)S(1)}, f32[2048,128]{1,0:T(8,128)S(1)}, u32[]{:S(2)}, u32[]{:S(2)}) collective-permute-start(f32[2048,128]{1,0:T(8,128)S(1)} %bitcast.70), channel_id=1, source_target_pairs={{2,0},{4,2},{6,4},{7,6},{5,7},{3,5},{1,3},{0,1},{10,8},{12,10},{14... | collective-permute-start | bytes 3145736 | tf_op jit(solution)/shard_map/ppermute | solution.py:264
  5.6 24.9 %collective-permute-start = (f32[2048,128]{1,0:T(8,128)S(1)}, f32[2048,128]{1,0:T(8,128)S(1)}, u32[]{:S(2)}, u32[]{:S(2)}) collective-permute-start(f32[2048,128]{1,0:T(8,128)S(1)} %bitcast.71), channel_id=1, source_target_pairs={{0,2},{2,4},{4,6},{6,7},{7,5},{5,3},{3,1},{1,0},{8,10},{10,12},{12... | collective-permute-start | bytes 3145736 | tf_op jit(solution)/shard_map/ppermute | solution.py:263
  28.8 18.6 %copy-start = (f32[2048,128]{1,0:T(8,128)}, f32[2048,128]{1,0:T(8,128)S(1)}, u32[]{:S(2)}) copy-start(f32[2048,128]{1,0:T(8,128)S(1)} %collective-permute-done.1.refs_2_) | copy-start | bytes 3145732
  28.8 24.4 %collective-permute-start.3 = (f32[2048,128]{1,0:T(8,128)S(1)}, f32[2048,128]{1,0:T(8,128)}, u32[]{:S(2)}, u32[]{:S(2)}) collective-permute-start(f32[2048,128]{1,0:T(8,128)S(1)} %collective-permute-done.1.refs_2_), channel_id=1, source_target_pairs={{2,0},{4,2},{6,4},{7,6},{5,7},{3,5},{1,3},{0,1},{10,8},{12,10},{14... | collective-permute-start | bytes 3145736 | tf_op jit(solution)/shard_map/ppermute | solution.py:264
  30.5 24.1 %collective-permute-start.2 = (f32[2048,128]{1,0:T(8,128)S(1)}, f32[2048,128]{1,0:T(8,128)}, u32[]{:S(2)}, u32[]{:S(2)}) collective-permute-start(f32[2048,128]{1,0:T(8,128)S(1)} %collective-permute-done.refs_1_), channel_id=1, source_target_pairs={{0,2},{2,4},{4,6},{6,7},{7,5},{5,3},{3,1},{1,0},{8,10},{10,12},{12... | collective-permute-start | bytes 3145736 | tf_op jit(solution)/shard_map/ppermute | solution.py:263
  30.9 1.0 copy-start.2
  32.7 22.7 %collective-permute-start.10 = (f32[2,512,128]{2,1,0:T(8,128)}, f32[2,512,128]{2,1,0:T(8,128)}, u32[]{:S(2)}, u32[]{:S(2)}) collective-permute-start(f32[2,512,128]{2,1,0:T(8,128)} %bitcast.67), channel_id=1, source_target_pairs={{0,8},{8,0},{16,24},{24,16},{1,9},{9,1},{17,25},{25,17},{2,10},{10... | collective-permute-start | bytes 1572872 | tf_op jit(solution)/shard_map/ppermute | solution.py:202
  32.7 14.7 %collective-permute-start.8 = (f32[2,512,128]{2,1,0:T(8,128)}, f32[2,512,128]{2,1,0:T(8,128)}, u32[]{:S(2)}, u32[]{:S(2)}) collective-permute-start(f32[2,512,128]{2,1,0:T(8,128)} %bitcast.67), channel_id=1, source_target_pairs={{0,16},{8,24},{16,0},{24,8},{1,17},{9,25},{17,1},{25,9},{2,18},{10... | collective-permute-start | bytes 1572872 | tf_op jit(solution)/shard_map/ppermute | solution.py:202
  47.3 9.3 %collective-permute-start.9 = (f32[2,512,128]{2,1,0:T(8,128)}, f32[2,512,128]{2,1,0:T(8,128)}, u32[]{:S(2)}, u32[]{:S(2)}) collective-permute-start(f32[2,512,128]{2,1,0:T(8,128)} %collective-permute-done.8), channel_id=1, source_target_pairs={{0,8},{8,0},{16,24},{24,16},{1,9},{9,1},{17,25},{25,17},{2,10},{10... | collective-permute-start | bytes 1572872 | tf_op jit(solution)/shard_map/ppermute | solution.py:202
  53.3 23.7 %collective-permute-start.5 = (f32[2048,128]{1,0:T(8,128)}, f32[2048,128]{1,0:T(8,128)S(1)}, u32[]{:S(2)}, u32[]{:S(2)}) collective-permute-start(f32[2048,128]{1,0:T(8,128)} %collective-permute-done.3.refs_4_), channel_id=1, source_target_pairs={{2,0},{4,2},{6,4},{7,6},{5,7},{3,5},{1,3},{0,1},{10,8},{12,10},{14... | collective-permute-start | bytes 3145736 | tf_op jit(solution)/shard_map/ppermute | solution.py:264
  54.7 23.5 %collective-permute-start.4 = (f32[2048,128]{1,0:T(8,128)}, f32[2048,128]{1,0:T(8,128)S(1)}, u32[]{:S(2)}, u32[]{:S(2)}) collective-permute-start(f32[2048,128]{1,0:T(8,128)} %collective-permute-done.2.refs_3_), channel_id=1, source_target_pairs={{0,2},{2,4},{4,6},{6,7},{7,5},{5,3},{3,1},{1,0},{8,10},{10,12},{12... | collective-permute-start | bytes 3145736 | tf_op jit(solution)/shard_map/ppermute | solution.py:263
  58.1 21.1 %copy-start.4 = (bf16[256,256]{1,0:T(8,128)(2,1)S(1)}, bf16[256,256]{1,0:T(8,128)(2,1)}, u32[]{:S(2)}) copy-start(bf16[256,256]{1,0:T(8,128)(2,1)} %constant.108.clone.refs_12_.refs_13_) | copy-start | bytes 393220
  58.1 21.1 %copy-start.5 = (bf16[256,256]{1,0:T(8,128)(2,1)S(1)}, bf16[256,256]{1,0:T(8,128)(2,1)}, u32[]{:S(2)}) copy-start(bf16[256,256]{1,0:T(8,128)(2,1)} %constant.107.clone.refs_11_.refs_12_) | copy-start | bytes 393220
  58.1 21.1 %copy-start.6 = (f32[64,128]{1,0:T(8,128)S(1)}, f32[64,128]{1,0:T(8,128)}, u32[]{:S(2)}) copy-start(f32[64,128]{1,0:T(8,128)} %constant.109.clone.refs_13_.refs_14_) | copy-start | bytes 98308
  58.1 21.0 %copy-start.7 = (bf16[128,128]{1,0:T(8,128)(2,1)S(1)}, bf16[128,128]{1,0:T(8,128)(2,1)}, u32[]{:S(2)}) copy-start(bf16[128,128]{1,0:T(8,128)(2,1)} %constant.106.clone.refs_10_.refs_11_) | copy-start | bytes 98308
  58.1 21.0 %copy-start.8 = (bf16[128,128]{1,0:T(8,128)(2,1)S(1)}, bf16[128,128]{1,0:T(8,128)(2,1)}, u32[]{:S(2)}) copy-start(bf16[128,128]{1,0:T(8,128)(2,1)} %constant.105.clone.refs_9_.refs_10_) | copy-start | bytes 98308
  58.1 21.0 %copy-start.9 = (bf16[128,128]{1,0:T(8,128)(2,1)S(1)}, bf16[128,128]{1,0:T(8,128)(2,1)}, u32[]{:S(2)}) copy-start(bf16[128,128]{1,0:T(8,128)(2,1)} %constant.104.clone.refs_8_.refs_9_) | copy-start | bytes 98308
  58.3 20.9 %copy-start.1 = (f32[2048,128]{1,0:T(8,128)S(1)}, f32[2048,128]{1,0:T(8,128)}, u32[]{:S(2)}) copy-start(f32[2048,128]{1,0:T(8,128)} %copy-done) | copy-start | bytes 3145732
  58.3 20.9 %copy-start.3 = (f32[2048,128]{1,0:T(8,128)S(1)}, f32[2048,128]{1,0:T(8,128)}, u32[]{:S(2)}) copy-start(f32[2048,128]{1,0:T(8,128)} %copy-done.2) | copy-start | bytes 3145732
  58.3 20.9 %copy-start.10 = (f32[64]{0:T(128)S(1)}, f32[64]{0:T(128)}, u32[]{:S(2)}) copy-start(f32[64]{0:T(128)} %constant.110.clone.wave) | copy-start | bytes 772
  77.0 37.7 %collective-permute-start.7 = (f32[1024,128]{1,0:T(8,128)S(1)}, f32[1024,128]{1,0:T(8,128)S(1)}, u32[]{:S(2)}, u32[]{:S(2)}) collective-permute-start(f32[1024,128]{1,0:T(8,128)S(1)} %slice.35), channel_id=1, source_target_pairs={{2,0},{4,2},{6,4},{7,6},{5,7},{3,5},{1,3},{0,1},{10,8},{12,10},{14... | collective-permute-start | bytes 1572872 | tf_op jit(solution)/shard_map/ppermute | solution.py:269
  78.2 36.4 %collective-permute-start.6 = (f32[1024,128]{1,0:T(8,128)S(1)}, f32[1024,128]{1,0:T(8,128)S(1)}, u32[]{:S(2)}, u32[]{:S(2)}) collective-permute-start(f32[1024,128]{1,0:T(8,128)S(1)} %slice.34), channel_id=1, source_target_pairs={{0,2},{2,4},{4,6},{6,7},{7,5},{5,3},{3,1},{1,0},{8,10},{10,12},{12... | collective-permute-start | bytes 1572872 | tf_op jit(solution)/shard_map/ppermute | solution.py:268
  114.6 1.3 copy-start.11
  152.6 2.7 %collective-permute-start.11 = (f32[2,2,512,128]{3,2,1,0:T(8,128)S(1)}, f32[2,2,512,128]{3,2,1,0:T(8,128)S(1)}, u32[]{:S(2)}, u32[]{:S(2)}) collective-permute-start(f32[2,2,512,128]{3,2,1,0:T(8,128)S(1)} %select_bitcast_fusion), channel_id=1, source_target_pairs={{0,8},{8,0},{16,24},{24,16},{1,9},{9,1},{17,25},{25,17},{2,10},{10... | collective-permute-start | bytes 3145736 | tf_op jit(solution)/shard_map/ppermute | solution.py:202
  155.6 14.0 %collective-permute-start.12 = (f32[2,1,512,128]{3,2,0,1:T(8,128)S(1)}, f32[2,1,512,128]{3,2,0,1:T(8,128)S(1)}, u32[]{:S(2)}, u32[]{:S(2)}) collective-permute-start(f32[2,1,512,128]{3,2,0,1:T(8,128)S(1)} %select_bitcast_fusion.1), channel_id=1, source_target_pairs={{0,16},{8,24},{16,0},{24,8},{1,17},{9,25},{17,1},{25,9},{2,18},{10... | collective-permute-start | bytes 1572872 | tf_op jit(solution)/shard_map/ppermute | solution.py:202

commit v2 on v1

--- a/solution.py
+++ b/solution.py
@@ -38,8 +38,7 @@
     along_x = stacked(cas)
     along_y = stacked(cas[:, order])
     back_y = stacked(cas[order, :])
-    blocks = np.kron(np.eye(4), cas)
-    z_high, z_low = split_np(blocks)
+    z_high, z_low = split_np(np.kron(np.eye(4), cas))
     freq = np.where(counter < NG // 2, counter, counter - NG)
     wave = (2.0 * np.pi * freq / box_length) ** 2
     plane = wave[:, None] + np.tile(wave, 2)[None, :] + screen_square
@@ -67,7 +66,9 @@
 
 
 HALF = NG // 2
-XB = 4
+XB = 8
+YB = 8
+CALLS = ((0, 1), (1, 3), (3, 4))
 
 
 def pair_kernel(count, has_prior, slots, wave, *refs):
@@ -78,13 +79,26 @@
     if has_prior:
         prior, refs = refs[0], refs[1:]
     out, src, field, sems = refs
-
-    for s in range(2):
+    ns = src.shape[0]
+    xb, yb = XB * 2 // ns, YB * 2 // ns
+    width = ns * LANES
+
+    def wide(parts):
+        return jnp.concatenate(parts, axis=1) if ns > 1 else parts[0]
+
+    def load(rows):
+        return wide([field[s, rows, :] for s in range(ns)])
+
+    def store(rows, v):
+        for s in range(ns):
+            field[s, rows, :] = v[:, s * LANES : (s + 1) * LANES]
+
+    for s in range(ns):
         for i in range(count):
             @pl.when(slots[s] == i)
             def _():
                 pltpu.make_async_copy(pool[i], src.at[s], sems.at[s]).start()
-    for s in range(2):
+    for s in range(ns):
         pltpu.make_async_copy(pool[0], src.at[s], sems.at[s]).wait()
 
     first = lax.broadcasted_iota(jnp.int32, (HALF, LANES), 1) < NG
@@ -100,47 +114,50 @@
         return jnp.concatenate([even, odd], axis=0)
 
     def source_plane(x):
-        return jnp.concatenate([source_rows(0, x), source_rows(1, x)], axis=1)
+        return wide([source_rows(s, x) for s in range(ns)])
 
     def forward(step, carry):
         slabs = []
-        for k in range(XB):
-            x = step * XB + k
+        for k in range(xb):
+            x = step * xb + k
             rows = pl.ds(pl.multiple_of(x * HALF, HALF), HALF)
             even, odd = interleave(targets[0, rows, :], targets[1, rows, :])
             t = jnp.concatenate([even, odd], axis=0)
-            slabs.append(jnp.concatenate([t, t], axis=1) * source_plane(x))
-        lines = right(z_high[...], z_low[...], jnp.concatenate(slabs, axis=0))
-        for k in range(XB):
-            x = step * XB + k
-            r = left(along_y[...], lines[k * NG : (k + 1) * NG])
+            slabs.append(wide([t] * ns) * source_plane(x))
+        lines = right(z_high[:width, :width], z_low[:width, :width], jnp.concatenate(slabs, axis=0))
+        for k in range(xb):
+            x = step * xb + k
             rows = pl.ds(pl.multiple_of(x * NG, NG), NG)
-            field[0, rows, :] = r[:, :LANES]
-            field[1, rows, :] = r[:, LANES:]
+            store(rows, left(along_y[...], lines[k * NG : (k + 1) * NG]))
         return carry
 
-    def middle(y, carry):
-        rows = pl.ds(y, NG, stride=NG)
-        v = jnp.concatenate([field[0, rows, :], field[1, rows, :]], axis=1)
-        v = left(along_x[...], v)
-        factor = (4.0 * math.pi) / (plane[...] + wave[y])
-        v = left(along_x[...], v * jnp.concatenate([factor, factor], axis=1))
-        field[0, rows, :] = v[:, :LANES]
-        field[1, rows, :] = v[:, LANES:]
+    def middle(step, carry):
+        group = [step * yb + k for k in range(yb)]
+        slabs = []
+        for y in group:
+            rows = pl.ds(y, NG, stride=NG)
+            slabs.append(load(rows))
+        slabs = [left(along_x[...], v) for v in slabs]
+        for k, y in enumerate(group):
+            factor = (4.0 * math.pi) / (plane[...] + wave[y])
+            slabs[k] = slabs[k] * wide([factor] * ns)
+        slabs = [left(along_x[...], v) for v in slabs]
+        for y, v in zip(group, slabs):
+            rows = pl.ds(y, NG, stride=NG)
+            store(rows, v)
         return carry
 
     def backward(step, carry):
         slabs = []
-        for k in range(XB):
-            x = step * XB + k
+        for k in range(xb):
+            x = step * xb + k
             rows = pl.ds(pl.multiple_of(x * NG, NG), NG)
-            v = jnp.concatenate([field[0, rows, :], field[1, rows, :]], axis=1)
-            slabs.append(left(back_y[...], v))
-        lines = right(z_high[...], z_low[...], jnp.concatenate(slabs, axis=0))
-        for k in range(XB):
-            x = step * XB + k
+            slabs.append(left(back_y[...], load(rows)))
+        lines = right(z_high[:width, :width], z_low[:width, :width], jnp.concatenate(slabs, axis=0))
+        for k in range(xb):
+            x = step * xb + k
             v = lines[k * NG : (k + 1) * NG] * source_plane(x)
-            v = v[:, :LANES] + v[:, LANES:]
+            v = sum(v[:, s * LANES : (s + 1) * LANES] for s in range(ns))
             a, b = interleave(v[:HALF], v[HALF:])
             rows = pl.ds(pl.multiple_of(x * HALF, HALF), HALF)
             if has_prior:
@@ -151,14 +168,15 @@
                 out[1, rows, :] = -b
         return carry
 
-    lax.fori_loop(0, NG // XB, forward, 0)
-    lax.fori_loop(0, NG, middle, 0, unroll=2)
-    lax.fori_loop(0, NG // XB, backward, 0)
+    lax.fori_loop(0, NG // xb, forward, 0)
+    lax.fori_loop(0, NG // yb, middle, 0)
+    lax.fori_loop(0, NG // xb, backward, 0)
 
 
 def exchange_terms(slots, pool, targets, prior, consts):
     *mats, wave = consts
     rows = targets.shape[1]
+    ns = slots.shape[0]
     smem = pl.BlockSpec(memory_space=pltpu.SMEM)
     vmem = pl.BlockSpec(memory_space=pltpu.VMEM)
     anywhere = pl.BlockSpec(memory_space=pl.ANY)
@@ -169,13 +187,13 @@
         in_specs=[smem, smem] + [anywhere] * len(pool) + [vmem] * (1 + len(mats) + len(extra)),
         out_specs=vmem,
         scratch_shapes=[
-            pltpu.VMEM((2, rows, LANES), jnp.float32),
-            pltpu.VMEM((2, NG * NG, LANES), jnp.float32),
-            pltpu.SemaphoreType.DMA((2,)),
+            pltpu.VMEM((ns, rows, LANES), jnp.float32),
+            pltpu.VMEM((ns, NG * NG, LANES), jnp.float32),
+            pltpu.SemaphoreType.DMA((ns,)),
         ],
         compiler_params=pltpu.CompilerParams(vmem_limit_bytes=40 * 1024 * 1024),
         cost_estimate=pl.CostEstimate(
-            flops=20_000_000_000, bytes_accessed=8_000_000, transcendentals=0
+            flops=10_000_000_000 * ns, bytes_accessed=8_000_000, transcendentals=0
         ),
     )(slots, wave, *pool, targets, *mats, *extra)
 
@@ -195,7 +213,7 @@
                 d = (place[b] - place[(b - off - k) % count]) % count
                 steps.append(min(d, count - d))
             worst = [max(w, s) for w, s in zip(worst, sorted(steps))]
-    return worst[1], worst[3]
+    return worst
 
 
 def partner(value, axis, bit):
@@ -255,7 +273,7 @@
     order = ring_order(count)
     up = [(order[i], order[(i + 1) % count]) for i in range(count)]
     down = [(b, a) for a, b in up]
-    first_step, last_step = arrival(count)
+    worst = arrival(count)
     pool = [scaled]
     ahead = behind = scaled
     for step in range(1, count // 2 + 1):
@@ -284,10 +302,10 @@
         jnp.where(rank[None, :] == jnp.arange(STOPS)[:, None], slot[None, :], 0), axis=1
     ).astype(jnp.int32)
 
-    early = pool[: 2 * first_step + 1]
-    late = pool[: 2 * last_step + 1]
-    partial = exchange_terms(ranked[:2], early, whole, None, consts)
-    total = exchange_terms(ranked[2:], late, whole, partial, consts)
+    total = None
+    for first, end in CALLS:
+        there = pool[: 2 * worst[end - 1] + 1]
+        total = exchange_terms(ranked[first:end], there, whole, total, consts)
     return scatter_rows(total, "grp").reshape(targets.shape)
 
 

time: 172 us -> 132 us (0.77)
  Pallas kernels: 71.9 us -> 43.2 us
  waiting for transfers between devices: 72.8 us -> 61.4 us
    ppermute x3, waiting for transfers between devices: 47.5 us -> 0.01 us  [local(): behind = lax.ppermute(behind, 'blk', down)]
    ppermute x3, waiting for transfers between devices: 0.01 us -> 37.2 us  [local(): ahead = lax.ppermute(ahead, 'blk', up)]
    pallas_call x2 -> x3, Pallas kernels: 71.9 us -> 43.2 us  [exchange_terms(): pl.pallas_call(functools.partial(pair_kernel, len(pool), prior is not Non...]
    ppermute x3, starting transfers between devices: 6.13 us -> 0.75 us  [local(): behind = lax.ppermute(behind, 'blk', down)]
    ppermute x3, starting transfers between devices: 1.09 us -> 6.42 us  [local(): ahead = lax.ppermute(ahead, 'blk', up)]
    unnamed x32 -> x24, local copies, waits for them, and re-layouts: 4.28 us -> 4.06 us
  transfers between devices with their start and end apart: 13 -> 13, of which waited for: 6 -> 6; matrix products, arithmetic and copies ran while one was open for 4% -> 6% of each run, Pallas kernels for 21% -> 24%
where the time goes in v2:
time: 132 us; the launch traced here: 131 us
  waiting for transfers between devices  61.4 us (47%)
  Pallas kernels  43.2 us (33%)
  starting transfers between devices  12.2 us (9%)
  local copies, waits for them, and re-layouts  6.81 us (5%)
  other arithmetic  6.14 us (5%)
  between operations  1.67 us (1%)
    pallas_call x3, Pallas kernels, exchange_terms(): pl.pallas_call(functools.partial(pair_kernel, len(pool), prior is not Non...  43.2 us
    ppermute x3, waiting for transfers between devices, local(): ahead = lax.ppermute(ahead, 'blk', up)  37.2 us
    ppermute x5, waiting for transfers between devices, partner(): lax.ppermute(value, axis, [(i, i ^ bit) for i in range(lax.axis_size(axis...  24.2 us
    ppermute x3, starting transfers between devices, local(): ahead = lax.ppermute(ahead, 'blk', up)  6.42 us
    unnamed x24, local copies, waits for them, and re-layouts  4.06 us
    ppermute x5, starting transfers between devices, partner(): lax.ppermute(value, axis, [(i, i ^ bit) for i in range(lax.axis_size(axis...  2.95 us
    select_n x3, other arithmetic, gather_rows(): jnp.where(swap, b, a)  2.68 us
  transfers between devices with their start and end apart: 13, of which 6 were waited for; matrix products, arithmetic and copies ran while one was open for 6% of the time, Pallas kernels for 24%

profile of v2, /device:TPU:0, one launch (start us, length us, event | category | flops | bytes accessed | tf_op | source)
XLA Modules:
  0.0 131.4 jit_solution(2678015453940227390)
XLA Ops:
  0.8 1.8 %broadcast_multiply_fusion = f32[1,262144]{1,0:T(1,128)S(1)} fusion(f32[1,262144]{1,0:T(1,128)} %param.13, f32[]{:T(128)} %bitcast.3), kind=kLoop, calls=%fused_computation.19 | loop fusion | flops 262144 | bytes 2097156 | tf_op jit(solution)/shard_map/mul | solution.py:268
  2.6 3.1 %collective-permute-start = (f32[2048,128]{1,0:T(8,128)S(1)}, f32[2048,128]{1,0:T(8,128)S(1)}, u32[]{:S(2)}, u32[]{:S(2)}) collective-permute-start(f32[2048,128]{1,0:T(8,128)S(1)} %bitcast.70), channel_id=1, source_target_pairs={{0,2},{2,4},{4,6},{6,7},{7,5},{5,3},{3,1},{1,0},{8,10},{10,12},{12... | collective-permute-start | bytes 3145736 | tf_op jit(solution)/shard_map/ppermute | solution.py:281
  5.7 0.0 collective-permute-start.1
  5.7 0.0 copy-done.9
  5.7 0.8 copy.48
  6.5 1.9 %collective-permute-start.8 = (f32[2,512,128]{2,1,0:T(8,128)}, f32[2,512,128]{2,1,0:T(8,128)}, u32[]{:S(2)}, u32[]{:S(2)}) collective-permute-start(f32[2,512,128]{2,1,0:T(8,128)} %bitcast.67), channel_id=1, source_target_pairs={{0,16},{8,24},{16,0},{24,8},{1,17},{9,25},{17,1},{25,9},{2,18},{10... | collective-permute-start | bytes 1572872 | tf_op jit(solution)/shard_map/ppermute | solution.py:220
  8.4 0.0 collective-permute-start.10
  8.4 0.0 copy-done.10
  8.4 0.6 dynamic_slice.8
  9.8 0.0 copy-done.8
  9.8 0.6 gather_fusion
  10.5 0.6 dynamic_slice.7
  11.1 0.7 compare_select_fusion.6
  11.8 8.4 %collective-permute-done.8 = f32[2,512,128]{2,1,0:T(8,128)} collective-permute-done((f32[2,512,128]{2,1,0:T(8,128)}, f32[2,512,128]{2,1,0:T(8,128)}, u32[]{:S(2)}, u32[]{:S(2)}) %collective-permute-start.8) | collective-permute-done | bytes 524320 | tf_op jit(solution)/shard_map/ppermute | solution.py:220
  20.2 0.0 collective-permute-start.9
  20.2 8.6 %collective-permute-done.refs_1_ = f32[2048,128]{1,0:T(8,128)S(1)} collective-permute-done((f32[2048,128]{1,0:T(8,128)S(1)}, f32[2048,128]{1,0:T(8,128)S(1)}, u32[]{:S(2)}, u32[]{:S(2)}) %collective-permute-start) | collective-permute-done | bytes 1048608 | tf_op jit(solution)/shard_map/ppermute | solution.py:281
  28.8 1.8 %collective-permute-start.2 = (f32[2048,128]{1,0:T(8,128)S(1)}, f32[2048,128]{1,0:T(8,128)}, u32[]{:S(2)}, u32[]{:S(2)}) collective-permute-start(f32[2048,128]{1,0:T(8,128)S(1)} %collective-permute-done.refs_1_), channel_id=1, source_target_pairs={{0,2},{2,4},{4,6},{6,7},{7,5},{5,3},{3,1},{1,0},{8,10},{10,12},{12... | collective-permute-start | bytes 3145736 | tf_op jit(solution)/shard_map/ppermute | solution.py:281
  30.6 0.0 collective-permute-done.1.refs_2_
  30.6 0.2 collective-permute-start.3
  30.8 0.2 convert_reduce_fusion
  31.0 0.1 select_reduce_fusion
  31.1 0.1 slice.30.slots
  31.2 0.7 fusion.11
  31.9 0.0 collective-permute-done.10
  31.9 1.3 broadcast_select_fusion.1
  33.2 0.0 collective-permute-done.9
  33.2 1.3 broadcast_select_fusion.3
  34.4 0.1 fusion.4
  34.6 18.6 %collective-permute-done.2.refs_3_ = f32[2048,128]{1,0:T(8,128)} collective-permute-done((f32[2048,128]{1,0:T(8,128)S(1)}, f32[2048,128]{1,0:T(8,128)}, u32[]{:S(2)}, u32[]{:S(2)}) %collective-permute-start.2) | collective-permute-done | bytes 1048608 | tf_op jit(solution)/shard_map/ppermute | solution.py:281
  53.2 1.5 %collective-permute-start.4 = (f32[2048,128]{1,0:T(8,128)}, f32[2048,128]{1,0:T(8,128)S(1)}, u32[]{:S(2)}, u32[]{:S(2)}) collective-permute-start(f32[2048,128]{1,0:T(8,128)} %collective-permute-done.2.refs_3_), channel_id=1, source_target_pairs={{0,2},{2,4},{4,6},{6,7},{7,5},{5,3},{3,1},{1,0},{8,10},{10,12},{12... | collective-permute-start | bytes 3145736 | tf_op jit(solution)/shard_map/ppermute | solution.py:281
  54.7 0.0 collective-permute-done.3.refs_4_
  54.7 0.5 collective-permute-start.5
  55.2 0.0 copy-start.4
  55.3 0.0 copy-start.5
  55.3 0.0 copy-start.6
  55.3 0.1 pad_maximum_fusion.refs_5_.refs_7_.refs_8_
  55.4 0.7 copy-done
  56.1 0.1 copy-done.1
  56.2 0.0 copy-done.2
  56.2 0.0 copy-done.3
  56.2 0.0 copy-done.4
  56.2 0.0 copy-done.5
  56.2 0.0 copy-done.6
  56.2 10.6 %shard_map.118.refs_14_ = f32[2,2048,128]{2,1,0:T(8,128)S(1)} custom-call(s32[1]{0:T(128)} %get-tuple-element.11.slots, f32[64]{0:T(128)S(1)} %copy-done.6, f32[2048,128]{1,0:T(8,128)S(1)} %bitcast.72, f32[2048,128]{1,0:T(8,128)S(1)} %collective-permute-done.refs_1_, f32[2048,128]{1,0:T(8,128)S(1)} %collective-permute-done.1.refs_2_, ...), custom_call_target="tpu_custom_call" | custom-call | flops 10000000000 | bytes 8000000 | tf_op jit(solution)/shard_map/pallas_call | solution.py:184
  66.9 10.0 %collective-permute-done.4.refs_5_ = f32[2048,128]{1,0:T(8,128)S(1)} collective-permute-done((f32[2048,128]{1,0:T(8,128)}, f32[2048,128]{1,0:T(8,128)S(1)}, u32[]{:S(2)}, u32[]{:S(2)}) %collective-permute-start.4) | collective-permute-done | bytes 1048608 | tf_op jit(solution)/shard_map/ppermute | solution.py:281
  76.9 1.3 %collective-permute-start.6 = (f32[1024,128]{1,0:T(8,128)S(1)}, f32[1024,128]{1,0:T(8,128)S(1)}, u32[]{:S(2)}, u32[]{:S(2)}) collective-permute-start(f32[1024,128]{1,0:T(8,128)S(1)} %slice.38), channel_id=1, source_target_pairs={{0,2},{2,4},{4,6},{6,7},{7,5},{5,3},{3,1},{1,0},{8,10},{10,12},{12... | collective-permute-start | bytes 1572872 | tf_op jit(solution)/shard_map/ppermute | solution.py:286
  78.3 0.0 collective-permute-done.5.refs_6_
  78.3 0.8 collective-permute-start.7
  79.1 20.7 %shard_map.119.refs_15_ = f32[2,2048,128]{2,1,0:T(8,128)S(1)} custom-call(s32[2]{0:T(128)S(1)} %slice.30.slots, f32[64]{0:T(128)S(1)} %copy-done.6, f32[2048,128]{1,0:T(8,128)S(1)} %bitcast.73, f32[2048,128]{1,0:T(8,128)S(1)} %collective-permute-done.refs_1_, f32[2048,128]{1,0:T(8,128)S(1)} %collective-permute-done.1.refs_2_, ...), custom_call_target="tpu_custom_call" | custom-call | flops 20000000000 | bytes 8000000 | tf_op jit(solution)/shard_map/pallas_call | solution.py:184
  99.8 0.0 copy-start.7
  99.8 0.0 collective-permute-done.6
  99.8 0.0 collective-permute-done.7
  99.9 0.1 pad_maximum_fusion.1.refs_7_
  99.9 1.2 copy-done.7
  101.2 11.8 %shard_map.120 = f32[2,2048,128]{2,1,0:T(8,128)S(1)} custom-call(s32[1]{0:T(128)} %get-tuple-element.12.slots, f32[64]{0:T(128)S(1)} %copy-done.6, f32[2048,128]{1,0:T(8,128)S(1)} %bitcast.74, f32[2048,128]{1,0:T(8,128)S(1)} %collective-permute-done.refs_1_, f32[2048,128]{1,0:T(8,128)S(1)} %collective-permute-done.1.refs_2_, ...), custom_call_target="tpu_custom_call" | custom-call | flops 10000000000 | bytes 8000000 | tf_op jit(solution)/shard_map/pallas_call | solution.py:184
  113.0 0.1 select_bitcast_fusion
  113.1 0.1 collective-permute-start.11
  113.2 2.6 %collective-permute-done.11 = f32[2,2,512,128]{3,2,1,0:T(8,128)S(1)} collective-permute-done((f32[2,2,512,128]{3,2,1,0:T(8,128)S(1)}, f32[2,2,512,128]{3,2,1,0:T(8,128)S(1)}, u32[]{:S(2)}, u32[]{:S(2)}) %collective-permute-start.11) | collective-permute-done | bytes 1048608 | tf_op jit(solution)/shard_map/ppermute | solution.py:220
  115.8 0.2 fusion.2
  116.0 0.1 select_bitcast_fusion.1
  116.1 0.9 collective-permute-start.12
  117.0 13.1 %collective-permute-done.12 = f32[2,1,512,128]{3,2,0,1:T(8,128)S(1)} collective-permute-done((f32[2,1,512,128]{3,2,0,1:T(8,128)S(1)}, f32[2,1,512,128]{3,2,0,1:T(8,128)S(1)}, u32[]{:S(2)}, u32[]{:S(2)}) %collective-permute-start.12) | collective-permute-done | bytes 524320 | tf_op jit(solution)/shard_map/ppermute | solution.py:220
  130.1 0.1 fusion.7
  130.2 1.2 copy.47
  (11 shorter events, 0.1 us)
Async XLA Ops:
  0.0 9.8 %copy-start.8 = (s32[8]{0:T(128)S(1)}, s32[8]{0:T(128)}, u32[]{:S(2)}) copy-start(s32[8]{0:T(128)} %constant.111.clone) | copy-start | bytes 100
  0.0 5.7 %copy-start.9 = (f32[2,65536]{1,0:T(2,128)S(1)}, f32[2,65536]{1,0:T(2,128)}, u32[]{:S(2)}) copy-start(f32[2,65536]{1,0:T(2,128)} %param.12) | copy-start | bytes 1572868
  0.0 8.4 %copy-start.10 = (s32[4]{0:T(128)S(1)}, s32[4]{0:T(128)}, u32[]{:S(2)}) copy-start(s32[4]{0:T(128)} %param.15) | copy-start | bytes 52
  2.6 26.2 %collective-permute-start = (f32[2048,128]{1,0:T(8,128)S(1)}, f32[2048,128]{1,0:T(8,128)S(1)}, u32[]{:S(2)}, u32[]{:S(2)}) collective-permute-start(f32[2048,128]{1,0:T(8,128)S(1)} %bitcast.70), channel_id=1, source_target_pairs={{0,2},{2,4},{4,6},{6,7},{7,5},{5,3},{3,1},{1,0},{8,10},{10,12},{12... | collective-permute-start | bytes 3145736 | tf_op jit(solution)/shard_map/ppermute | solution.py:281
  5.7 24.9 %collective-permute-start.1 = (f32[2048,128]{1,0:T(8,128)S(1)}, f32[2048,128]{1,0:T(8,128)S(1)}, u32[]{:S(2)}, u32[]{:S(2)}) collective-permute-start(f32[2048,128]{1,0:T(8,128)S(1)} %bitcast.71), channel_id=1, source_target_pairs={{2,0},{4,2},{6,4},{7,6},{5,7},{3,5},{1,3},{0,1},{10,8},{12,10},{14... | collective-permute-start | bytes 3145736 | tf_op jit(solution)/shard_map/ppermute | solution.py:282
  6.5 13.7 %collective-permute-start.8 = (f32[2,512,128]{2,1,0:T(8,128)}, f32[2,512,128]{2,1,0:T(8,128)}, u32[]{:S(2)}, u32[]{:S(2)}) collective-permute-start(f32[2,512,128]{2,1,0:T(8,128)} %bitcast.67), channel_id=1, source_target_pairs={{0,16},{8,24},{16,0},{24,8},{1,17},{9,25},{17,1},{25,9},{2,18},{10... | collective-permute-start | bytes 1572872 | tf_op jit(solution)/shard_map/ppermute | solution.py:220
  8.4 23.4 %collective-permute-start.10 = (f32[2,512,128]{2,1,0:T(8,128)}, f32[2,512,128]{2,1,0:T(8,128)}, u32[]{:S(2)}, u32[]{:S(2)}) collective-permute-start(f32[2,512,128]{2,1,0:T(8,128)} %bitcast.67), channel_id=1, source_target_pairs={{0,8},{8,0},{16,24},{24,16},{1,9},{9,1},{17,25},{25,17},{2,10},{10... | collective-permute-start | bytes 1572872 | tf_op jit(solution)/shard_map/ppermute | solution.py:220
  20.2 12.9 %collective-permute-start.9 = (f32[2,512,128]{2,1,0:T(8,128)}, f32[2,512,128]{2,1,0:T(8,128)}, u32[]{:S(2)}, u32[]{:S(2)}) collective-permute-start(f32[2,512,128]{2,1,0:T(8,128)} %collective-permute-done.8), channel_id=1, source_target_pairs={{0,8},{8,0},{16,24},{24,16},{1,9},{9,1},{17,25},{25,17},{2,10},{10... | collective-permute-start | bytes 1572872 | tf_op jit(solution)/shard_map/ppermute | solution.py:220
  28.8 24.4 %collective-permute-start.2 = (f32[2048,128]{1,0:T(8,128)S(1)}, f32[2048,128]{1,0:T(8,128)}, u32[]{:S(2)}, u32[]{:S(2)}) collective-permute-start(f32[2048,128]{1,0:T(8,128)S(1)} %collective-permute-done.refs_1_), channel_id=1, source_target_pairs={{0,2},{2,4},{4,6},{6,7},{7,5},{5,3},{3,1},{1,0},{8,10},{10,12},{12... | collective-permute-start | bytes 3145736 | tf_op jit(solution)/shard_map/ppermute | solution.py:281
  30.6 24.1 %collective-permute-start.3 = (f32[2048,128]{1,0:T(8,128)S(1)}, f32[2048,128]{1,0:T(8,128)}, u32[]{:S(2)}, u32[]{:S(2)}) collective-permute-start(f32[2048,128]{1,0:T(8,128)S(1)} %collective-permute-done.1.refs_2_), channel_id=1, source_target_pairs={{2,0},{4,2},{6,4},{7,6},{5,7},{3,5},{1,3},{0,1},{10,8},{12,10},{14... | collective-permute-start | bytes 3145736 | tf_op jit(solution)/shard_map/ppermute | solution.py:282
  53.2 23.7 %collective-permute-start.4 = (f32[2048,128]{1,0:T(8,128)}, f32[2048,128]{1,0:T(8,128)S(1)}, u32[]{:S(2)}, u32[]{:S(2)}) collective-permute-start(f32[2048,128]{1,0:T(8,128)} %collective-permute-done.2.refs_3_), channel_id=1, source_target_pairs={{0,2},{2,4},{4,6},{6,7},{7,5},{5,3},{3,1},{1,0},{8,10},{10,12},{12... | collective-permute-start | bytes 3145736 | tf_op jit(solution)/shard_map/ppermute | solution.py:281
  54.7 23.5 %collective-permute-start.5 = (f32[2048,128]{1,0:T(8,128)}, f32[2048,128]{1,0:T(8,128)S(1)}, u32[]{:S(2)}, u32[]{:S(2)}) collective-permute-start(f32[2048,128]{1,0:T(8,128)} %collective-permute-done.3.refs_4_), channel_id=1, source_target_pairs={{2,0},{4,2},{6,4},{7,6},{5,7},{3,5},{1,3},{0,1},{10,8},{12,10},{14... | collective-permute-start | bytes 3145736 | tf_op jit(solution)/shard_map/ppermute | solution.py:282
  55.2 0.9 copy-start
  55.2 1.0 copy-start.1
  55.2 1.0 copy-start.2
  55.2 1.0 copy-start.3
  55.2 1.0 copy-start.4
  55.3 1.0 copy-start.5
  55.3 0.9 copy-start.6
  76.9 22.9 %collective-permute-start.6 = (f32[1024,128]{1,0:T(8,128)S(1)}, f32[1024,128]{1,0:T(8,128)S(1)}, u32[]{:S(2)}, u32[]{:S(2)}) collective-permute-start(f32[1024,128]{1,0:T(8,128)S(1)} %slice.38), channel_id=1, source_target_pairs={{0,2},{2,4},{4,6},{6,7},{7,5},{5,3},{3,1},{1,0},{8,10},{10,12},{12... | collective-permute-start | bytes 1572872 | tf_op jit(solution)/shard_map/ppermute | solution.py:286
  78.3 21.6 %collective-permute-start.7 = (f32[1024,128]{1,0:T(8,128)S(1)}, f32[1024,128]{1,0:T(8,128)S(1)}, u32[]{:S(2)}, u32[]{:S(2)}) collective-permute-start(f32[1024,128]{1,0:T(8,128)S(1)} %slice.39), channel_id=1, source_target_pairs={{2,0},{4,2},{6,4},{7,6},{5,7},{3,5},{1,3},{0,1},{10,8},{12,10},{14... | collective-permute-start | bytes 1572872 | tf_op jit(solution)/shard_map/ppermute | solution.py:287
  99.8 1.3 %copy-start.7 = (f32[2,2048,128]{2,1,0:T(8,128)}, f32[2,2048,128]{2,1,0:T(8,128)S(1)}, u32[]{:S(2)}) copy-start(f32[2,2048,128]{2,1,0:T(8,128)S(1)} %shard_map.119.refs_15_) | copy-start | bytes 6291460
  113.1 2.7 %collective-permute-start.11 = (f32[2,2,512,128]{3,2,1,0:T(8,128)S(1)}, f32[2,2,512,128]{3,2,1,0:T(8,128)S(1)}, u32[]{:S(2)}, u32[]{:S(2)}) collective-permute-start(f32[2,2,512,128]{3,2,1,0:T(8,128)S(1)} %select_bitcast_fusion), channel_id=1, source_target_pairs={{0,8},{8,0},{16,24},{24,16},{1,9},{9,1},{17,25},{25,17},{2,10},{10... | collective-permute-start | bytes 3145736 | tf_op jit(solution)/shard_map/ppermute | solution.py:220
  116.1 14.0 %collective-permute-start.12 = (f32[2,1,512,128]{3,2,0,1:T(8,128)S(1)}, f32[2,1,512,128]{3,2,0,1:T(8,128)S(1)}, u32[]{:S(2)}, u32[]{:S(2)}) collective-permute-start(f32[2,1,512,128]{3,2,0,1:T(8,128)S(1)} %select_bitcast_fusion.1), channel_id=1, source_target_pairs={{0,16},{8,24},{16,0},{24,8},{1,17},{9,25},{17,1},{25,9},{2,18},{10... | collective-permute-start | bytes 1572872 | tf_op jit(solution)/shard_map/ppermute | solution.py:220

commit v3 on v2

--- a/solution.py
+++ b/solution.py
@@ -66,7 +66,7 @@
 
 
 HALF = NG // 2
-XB = 8
+XB = 16
 YB = 8
 CALLS = ((0, 1), (1, 3), (3, 4))
 

time: 132 us -> 128 us (0.970)
  Pallas kernels: 43.2 us -> 38.7 us
  starting transfers between devices: 12.2 us -> 13.9 us
    pallas_call x3, Pallas kernels: 43.2 us -> 38.7 us  [exchange_terms(): pl.pallas_call(functools.partial(pair_kernel, len(pool), prior is not Non...]
    ppermute x5, starting transfers between devices: 2.95 us -> 4.62 us  [partner(): lax.ppermute(value, axis, [(i, i ^ bit) for i in range(lax.axis_size(axis...]
  transfers between devices with their start and end apart: 13 -> 13, of which waited for: 6 -> 6; matrix products, arithmetic and copies ran while one was open for 6% -> 6% of each run, Pallas kernels for 24% -> 22%
where the time goes in v3:
time: 128 us
  waiting for transfers between devices  60.4 us (47%)
  Pallas kernels  38.7 us (30%)
  starting transfers between devices  13.9 us (11%)
  local copies, waits for them, and re-layouts  6.81 us (5%)
  other arithmetic  6.14 us (5%)
  between operations  1.67 us (1%)
    pallas_call x3, Pallas kernels, exchange_terms(): pl.pallas_call(functools.partial(pair_kernel, len(pool), prior is not Non...  38.7 us
    ppermute x3, waiting for transfers between devices, local(): ahead = lax.ppermute(ahead, 'blk', up)  37.1 us
    ppermute x5, waiting for transfers between devices, partner(): lax.ppermute(value, axis, [(i, i ^ bit) for i in range(lax.axis_size(axis...  23.3 us
    ppermute x3, starting transfers between devices, local(): ahead = lax.ppermute(ahead, 'blk', up)  6.42 us
    ppermute x5, starting transfers between devices, partner(): lax.ppermute(value, axis, [(i, i ^ bit) for i in range(lax.axis_size(axis...  4.62 us
    unnamed x24, local copies, waits for them, and re-layouts  4.06 us
    select_n x3, other arithmetic, gather_rows(): jnp.where(swap, b, a)  2.68 us
  transfers between devices with their start and end apart: 13, of which 6 were waited for; matrix products, arithmetic and copies ran while one was open for 6% of the time, Pallas kernels for 22%

profile of v3, /device:TPU:0, one launch (start us, length us, event | category | flops | bytes accessed | tf_op | source)
XLA Modules:
  0.0 127.7 jit_solution(5030749626897053503)
XLA Ops:
  0.8 1.8 %broadcast_multiply_fusion = f32[1,262144]{1,0:T(1,128)S(1)} fusion(f32[1,262144]{1,0:T(1,128)} %param.13, f32[]{:T(128)} %bitcast.3), kind=kLoop, calls=%fused_computation.19 | loop fusion | flops 262144 | bytes 2097156 | tf_op jit(solution)/shard_map/mul | solution.py:268
  2.6 3.1 %collective-permute-start = (f32[2048,128]{1,0:T(8,128)S(1)}, f32[2048,128]{1,0:T(8,128)S(1)}, u32[]{:S(2)}, u32[]{:S(2)}) collective-permute-start(f32[2048,128]{1,0:T(8,128)S(1)} %bitcast.70), channel_id=1, source_target_pairs={{0,2},{2,4},{4,6},{6,7},{7,5},{5,3},{3,1},{1,0},{8,10},{10,12},{12... | collective-permute-start | bytes 3145736 | tf_op jit(solution)/shard_map/ppermute | solution.py:281
  5.7 0.0 collective-permute-start.1
  5.7 0.0 copy-done.9
  5.7 0.8 copy.48
  6.5 1.9 %collective-permute-start.8 = (f32[2,512,128]{2,1,0:T(8,128)}, f32[2,512,128]{2,1,0:T(8,128)}, u32[]{:S(2)}, u32[]{:S(2)}) collective-permute-start(f32[2,512,128]{2,1,0:T(8,128)} %bitcast.67), channel_id=1, source_target_pairs={{0,16},{8,24},{16,0},{24,8},{1,17},{9,25},{17,1},{25,9},{2,18},{10... | collective-permute-start | bytes 1572872 | tf_op jit(solution)/shard_map/ppermute | solution.py:220
  8.4 0.0 collective-permute-start.10
  8.4 0.0 copy-done.10
  8.4 0.6 dynamic_slice.8
  9.8 0.0 copy-done.8
  9.8 0.6 gather_fusion
  10.5 0.6 dynamic_slice.7
  11.1 0.7 compare_select_fusion.6
  11.8 8.4 %collective-permute-done.8 = f32[2,512,128]{2,1,0:T(8,128)} collective-permute-done((f32[2,512,128]{2,1,0:T(8,128)}, f32[2,512,128]{2,1,0:T(8,128)}, u32[]{:S(2)}, u32[]{:S(2)}) %collective-permute-start.8) | collective-permute-done | bytes 524320 | tf_op jit(solution)/shard_map/ppermute | solution.py:220
  20.2 0.0 collective-permute-start.9
  20.2 8.6 %collective-permute-done.refs_1_ = f32[2048,128]{1,0:T(8,128)S(1)} collective-permute-done((f32[2048,128]{1,0:T(8,128)S(1)}, f32[2048,128]{1,0:T(8,128)S(1)}, u32[]{:S(2)}, u32[]{:S(2)}) %collective-permute-start) | collective-permute-done | bytes 1048608 | tf_op jit(solution)/shard_map/ppermute | solution.py:281
  28.8 1.8 %collective-permute-start.2 = (f32[2048,128]{1,0:T(8,128)S(1)}, f32[2048,128]{1,0:T(8,128)}, u32[]{:S(2)}, u32[]{:S(2)}) collective-permute-start(f32[2048,128]{1,0:T(8,128)S(1)} %collective-permute-done.refs_1_), channel_id=1, source_target_pairs={{0,2},{2,4},{4,6},{6,7},{7,5},{5,3},{3,1},{1,0},{8,10},{10,12},{12... | collective-permute-start | bytes 3145736 | tf_op jit(solution)/shard_map/ppermute | solution.py:281
  30.6 0.0 collective-permute-done.1.refs_2_
  30.6 0.2 collective-permute-start.3
  30.8 0.2 convert_reduce_fusion
  31.0 0.1 select_reduce_fusion
  31.1 0.1 slice.30.slots
  31.2 0.7 fusion.11
  31.9 0.0 collective-permute-done.10
  31.9 1.3 broadcast_select_fusion.1
  33.2 0.0 collective-permute-done.9
  33.2 1.3 broadcast_select_fusion.3
  34.4 0.1 fusion.4
  34.6 18.6 %collective-permute-done.2.refs_3_ = f32[2048,128]{1,0:T(8,128)} collective-permute-done((f32[2048,128]{1,0:T(8,128)S(1)}, f32[2048,128]{1,0:T(8,128)}, u32[]{:S(2)}, u32[]{:S(2)}) %collective-permute-start.2) | collective-permute-done | bytes 1048608 | tf_op jit(solution)/shard_map/ppermute | solution.py:281
  53.2 1.5 %collective-permute-start.4 = (f32[2048,128]{1,0:T(8,128)}, f32[2048,128]{1,0:T(8,128)S(1)}, u32[]{:S(2)}, u32[]{:S(2)}) collective-permute-start(f32[2048,128]{1,0:T(8,128)} %collective-permute-done.2.refs_3_), channel_id=1, source_target_pairs={{0,2},{2,4},{4,6},{6,7},{7,5},{5,3},{3,1},{1,0},{8,10},{10,12},{12... | collective-permute-start | bytes 3145736 | tf_op jit(solution)/shard_map/ppermute | solution.py:281
  54.7 0.0 collective-permute-done.3.refs_4_
  54.7 0.5 collective-permute-start.5
  55.2 0.0 copy-start.4
  55.3 0.0 copy-start.5
  55.3 0.0 copy-start.6
  55.3 0.1 pad_maximum_fusion.refs_5_.refs_7_.refs_8_
  55.4 0.7 copy-done
  56.1 0.1 copy-done.1
  56.2 0.0 copy-done.2
  56.2 0.0 copy-done.3
  56.2 0.0 copy-done.4
  56.2 0.0 copy-done.5
  56.2 0.0 copy-done.6
  56.2 10.7 %shard_map.118.refs_14_ = f32[2,2048,128]{2,1,0:T(8,128)S(1)} custom-call(s32[1]{0:T(128)} %get-tuple-element.11.slots, f32[64]{0:T(128)S(1)} %copy-done.6, f32[2048,128]{1,0:T(8,128)S(1)} %bitcast.72, f32[2048,128]{1,0:T(8,128)S(1)} %collective-permute-done.refs_1_, f32[2048,128]{1,0:T(8,128)S(1)} %collective-permute-done.1.refs_2_, ...), custom_call_target="tpu_custom_call" | custom-call | flops 10000000000 | bytes 8000000 | tf_op jit(solution)/shard_map/pallas_call | solution.py:184
  66.9 9.9 %collective-permute-done.4.refs_5_ = f32[2048,128]{1,0:T(8,128)S(1)} collective-permute-done((f32[2048,128]{1,0:T(8,128)}, f32[2048,128]{1,0:T(8,128)S(1)}, u32[]{:S(2)}, u32[]{:S(2)}) %collective-permute-start.4) | collective-permute-done | bytes 1048608 | tf_op jit(solution)/shard_map/ppermute | solution.py:281
  76.9 1.3 %collective-permute-start.6 = (f32[1024,128]{1,0:T(8,128)S(1)}, f32[1024,128]{1,0:T(8,128)S(1)}, u32[]{:S(2)}, u32[]{:S(2)}) collective-permute-start(f32[1024,128]{1,0:T(8,128)S(1)} %slice.38), channel_id=1, source_target_pairs={{0,2},{2,4},{4,6},{6,7},{7,5},{5,3},{3,1},{1,0},{8,10},{10,12},{12... | collective-permute-start | bytes 1572872 | tf_op jit(solution)/shard_map/ppermute | solution.py:286
  78.3 0.0 collective-permute-done.5.refs_6_
  78.3 0.8 collective-permute-start.7
  79.1 17.1 %shard_map.119.refs_15_ = f32[2,2048,128]{2,1,0:T(8,128)S(1)} custom-call(s32[2]{0:T(128)S(1)} %slice.30.slots, f32[64]{0:T(128)S(1)} %copy-done.6, f32[2048,128]{1,0:T(8,128)S(1)} %bitcast.73, f32[2048,128]{1,0:T(8,128)S(1)} %collective-permute-done.refs_1_, f32[2048,128]{1,0:T(8,128)S(1)} %collective-permute-done.1.refs_2_, ...), custom_call_target="tpu_custom_call" | custom-call | flops 20000000000 | bytes 8000000 | tf_op jit(solution)/shard_map/pallas_call | solution.py:184
  96.2 0.0 copy-start.7
  96.3 0.0 collective-permute-done.6
  96.3 0.0 collective-permute-done.7
  96.3 0.1 pad_maximum_fusion.1.refs_7_
  96.4 1.2 copy-done.7
  97.6 10.9 %shard_map.120 = f32[2,2048,128]{2,1,0:T(8,128)S(1)} custom-call(s32[1]{0:T(128)} %get-tuple-element.12.slots, f32[64]{0:T(128)S(1)} %copy-done.6, f32[2048,128]{1,0:T(8,128)S(1)} %bitcast.74, f32[2048,128]{1,0:T(8,128)S(1)} %collective-permute-done.refs_1_, f32[2048,128]{1,0:T(8,128)S(1)} %collective-permute-done.1.refs_2_, ...), custom_call_target="tpu_custom_call" | custom-call | flops 10000000000 | bytes 8000000 | tf_op jit(solution)/shard_map/pallas_call | solution.py:184
  108.5 0.1 select_bitcast_fusion
  108.6 0.1 collective-permute-start.11
  108.7 2.6 %collective-permute-done.11 = f32[2,2,512,128]{3,2,1,0:T(8,128)S(1)} collective-permute-done((f32[2,2,512,128]{3,2,1,0:T(8,128)S(1)}, f32[2,2,512,128]{3,2,1,0:T(8,128)S(1)}, u32[]{:S(2)}, u32[]{:S(2)}) %collective-permute-start.11) | collective-permute-done | bytes 1048608 | tf_op jit(solution)/shard_map/ppermute | solution.py:220
  111.3 0.2 fusion.2
  111.5 0.1 select_bitcast_fusion.1
  111.6 2.6 %collective-permute-start.12 = (f32[2,1,512,128]{3,2,0,1:T(8,128)S(1)}, f32[2,1,512,128]{3,2,0,1:T(8,128)S(1)}, u32[]{:S(2)}, u32[]{:S(2)}) collective-permute-start(f32[2,1,512,128]{3,2,0,1:T(8,128)S(1)} %select_bitcast_fusion.1), channel_id=1, source_target_pairs={{0,16},{8,24},{16,0},{24,8},{1,17},{9,25},{17,1},{25,9},{2,18},{10... | collective-permute-start | bytes 1572872 | tf_op jit(solution)/shard_map/ppermute | solution.py:220
  114.2 12.2 %collective-permute-done.12 = f32[2,1,512,128]{3,2,0,1:T(8,128)S(1)} collective-permute-done((f32[2,1,512,128]{3,2,0,1:T(8,128)S(1)}, f32[2,1,512,128]{3,2,0,1:T(8,128)S(1)}, u32[]{:S(2)}, u32[]{:S(2)}) %collective-permute-start.12) | collective-permute-done | bytes 524320 | tf_op jit(solution)/shard_map/ppermute | solution.py:220
  126.4 0.1 fusion.7
  126.5 1.2 copy.47
  (11 shorter events, 0.1 us)
Async XLA Ops:
  0.0 9.8 %copy-start.8 = (s32[8]{0:T(128)S(1)}, s32[8]{0:T(128)}, u32[]{:S(2)}) copy-start(s32[8]{0:T(128)} %constant.111.clone) | copy-start | bytes 100
  0.0 5.7 %copy-start.9 = (f32[2,65536]{1,0:T(2,128)S(1)}, f32[2,65536]{1,0:T(2,128)}, u32[]{:S(2)}) copy-start(f32[2,65536]{1,0:T(2,128)} %param.12) | copy-start | bytes 1572868
  0.0 8.4 %copy-start.10 = (s32[4]{0:T(128)S(1)}, s32[4]{0:T(128)}, u32[]{:S(2)}) copy-start(s32[4]{0:T(128)} %param.15) | copy-start | bytes 52
  2.6 26.2 %collective-permute-start = (f32[2048,128]{1,0:T(8,128)S(1)}, f32[2048,128]{1,0:T(8,128)S(1)}, u32[]{:S(2)}, u32[]{:S(2)}) collective-permute-start(f32[2048,128]{1,0:T(8,128)S(1)} %bitcast.70), channel_id=1, source_target_pairs={{0,2},{2,4},{4,6},{6,7},{7,5},{5,3},{3,1},{1,0},{8,10},{10,12},{12... | collective-permute-start | bytes 3145736 | tf_op jit(solution)/shard_map/ppermute | solution.py:281
  5.7 24.9 %collective-permute-start.1 = (f32[2048,128]{1,0:T(8,128)S(1)}, f32[2048,128]{1,0:T(8,128)S(1)}, u32[]{:S(2)}, u32[]{:S(2)}) collective-permute-start(f32[2048,128]{1,0:T(8,128)S(1)} %bitcast.71), channel_id=1, source_target_pairs={{2,0},{4,2},{6,4},{7,6},{5,7},{3,5},{1,3},{0,1},{10,8},{12,10},{14... | collective-permute-start | bytes 3145736 | tf_op jit(solution)/shard_map/ppermute | solution.py:282
  6.5 13.7 %collective-permute-start.8 = (f32[2,512,128]{2,1,0:T(8,128)}, f32[2,512,128]{2,1,0:T(8,128)}, u32[]{:S(2)}, u32[]{:S(2)}) collective-permute-start(f32[2,512,128]{2,1,0:T(8,128)} %bitcast.67), channel_id=1, source_target_pairs={{0,16},{8,24},{16,0},{24,8},{1,17},{9,25},{17,1},{25,9},{2,18},{10... | collective-permute-start | bytes 1572872 | tf_op jit(solution)/shard_map/ppermute | solution.py:220
  8.4 23.4 %collective-permute-start.10 = (f32[2,512,128]{2,1,0:T(8,128)}, f32[2,512,128]{2,1,0:T(8,128)}, u32[]{:S(2)}, u32[]{:S(2)}) collective-permute-start(f32[2,512,128]{2,1,0:T(8,128)} %bitcast.67), channel_id=1, source_target_pairs={{0,8},{8,0},{16,24},{24,16},{1,9},{9,1},{17,25},{25,17},{2,10},{10... | collective-permute-start | bytes 1572872 | tf_op jit(solution)/shard_map/ppermute | solution.py:220
  20.2 12.9 %collective-permute-start.9 = (f32[2,512,128]{2,1,0:T(8,128)}, f32[2,512,128]{2,1,0:T(8,128)}, u32[]{:S(2)}, u32[]{:S(2)}) collective-permute-start(f32[2,512,128]{2,1,0:T(8,128)} %collective-permute-done.8), channel_id=1, source_target_pairs={{0,8},{8,0},{16,24},{24,16},{1,9},{9,1},{17,25},{25,17},{2,10},{10... | collective-permute-start | bytes 1572872 | tf_op jit(solution)/shard_map/ppermute | solution.py:220
  28.8 24.4 %collective-permute-start.2 = (f32[2048,128]{1,0:T(8,128)S(1)}, f32[2048,128]{1,0:T(8,128)}, u32[]{:S(2)}, u32[]{:S(2)}) collective-permute-start(f32[2048,128]{1,0:T(8,128)S(1)} %collective-permute-done.refs_1_), channel_id=1, source_target_pairs={{0,2},{2,4},{4,6},{6,7},{7,5},{5,3},{3,1},{1,0},{8,10},{10,12},{12... | collective-permute-start | bytes 3145736 | tf_op jit(solution)/shard_map/ppermute | solution.py:281
  30.6 24.1 %collective-permute-start.3 = (f32[2048,128]{1,0:T(8,128)S(1)}, f32[2048,128]{1,0:T(8,128)}, u32[]{:S(2)}, u32[]{:S(2)}) collective-permute-start(f32[2048,128]{1,0:T(8,128)S(1)} %collective-permute-done.1.refs_2_), channel_id=1, source_target_pairs={{2,0},{4,2},{6,4},{7,6},{5,7},{3,5},{1,3},{0,1},{10,8},{12,10},{14... | collective-permute-start | bytes 3145736 | tf_op jit(solution)/shard_map/ppermute | solution.py:282
  53.2 23.7 %collective-permute-start.4 = (f32[2048,128]{1,0:T(8,128)}, f32[2048,128]{1,0:T(8,128)S(1)}, u32[]{:S(2)}, u32[]{:S(2)}) collective-permute-start(f32[2048,128]{1,0:T(8,128)} %collective-permute-done.2.refs_3_), channel_id=1, source_target_pairs={{0,2},{2,4},{4,6},{6,7},{7,5},{5,3},{3,1},{1,0},{8,10},{10,12},{12... | collective-permute-start | bytes 3145736 | tf_op jit(solution)/shard_map/ppermute | solution.py:281
  54.7 23.5 %collective-permute-start.5 = (f32[2048,128]{1,0:T(8,128)}, f32[2048,128]{1,0:T(8,128)S(1)}, u32[]{:S(2)}, u32[]{:S(2)}) collective-permute-start(f32[2048,128]{1,0:T(8,128)} %collective-permute-done.3.refs_4_), channel_id=1, source_target_pairs={{2,0},{4,2},{6,4},{7,6},{5,7},{3,5},{1,3},{0,1},{10,8},{12,10},{14... | collective-permute-start | bytes 3145736 | tf_op jit(solution)/shard_map/ppermute | solution.py:282
  55.2 0.9 copy-start
  55.2 1.0 copy-start.1
  55.2 1.0 copy-start.2
  55.2 1.0 copy-start.3
  55.2 1.0 copy-start.4
  55.3 1.0 copy-start.5
  55.3 0.9 copy-start.6
  76.9 19.3 %collective-permute-start.6 = (f32[1024,128]{1,0:T(8,128)S(1)}, f32[1024,128]{1,0:T(8,128)S(1)}, u32[]{:S(2)}, u32[]{:S(2)}) collective-permute-start(f32[1024,128]{1,0:T(8,128)S(1)} %slice.38), channel_id=1, source_target_pairs={{0,2},{2,4},{4,6},{6,7},{7,5},{5,3},{3,1},{1,0},{8,10},{10,12},{12... | collective-permute-start | bytes 1572872 | tf_op jit(solution)/shard_map/ppermute | solution.py:286
  78.3 18.0 %collective-permute-start.7 = (f32[1024,128]{1,0:T(8,128)S(1)}, f32[1024,128]{1,0:T(8,128)S(1)}, u32[]{:S(2)}, u32[]{:S(2)}) collective-permute-start(f32[1024,128]{1,0:T(8,128)S(1)} %slice.39), channel_id=1, source_target_pairs={{2,0},{4,2},{6,4},{7,6},{5,7},{3,5},{1,3},{0,1},{10,8},{12,10},{14... | collective-permute-start | bytes 1572872 | tf_op jit(solution)/shard_map/ppermute | solution.py:287
  96.2 1.3 %copy-start.7 = (f32[2,2048,128]{2,1,0:T(8,128)}, f32[2,2048,128]{2,1,0:T(8,128)S(1)}, u32[]{:S(2)}) copy-start(f32[2,2048,128]{2,1,0:T(8,128)S(1)} %shard_map.119.refs_15_) | copy-start | bytes 6291460
  108.6 2.7 %collective-permute-start.11 = (f32[2,2,512,128]{3,2,1,0:T(8,128)S(1)}, f32[2,2,512,128]{3,2,1,0:T(8,128)S(1)}, u32[]{:S(2)}, u32[]{:S(2)}) collective-permute-start(f32[2,2,512,128]{3,2,1,0:T(8,128)S(1)} %select_bitcast_fusion), channel_id=1, source_target_pairs={{0,8},{8,0},{16,24},{24,16},{1,9},{9,1},{17,25},{25,17},{2,10},{10... | collective-permute-start | bytes 3145736 | tf_op jit(solution)/shard_map/ppermute | solution.py:220
  111.6 14.8 %collective-permute-start.12 = (f32[2,1,512,128]{3,2,0,1:T(8,128)S(1)}, f32[2,1,512,128]{3,2,0,1:T(8,128)S(1)}, u32[]{:S(2)}, u32[]{:S(2)}) collective-permute-start(f32[2,1,512,128]{3,2,0,1:T(8,128)S(1)} %select_bitcast_fusion.1), channel_id=1, source_target_pairs={{0,16},{8,24},{16,0},{24,8},{1,17},{9,25},{17,1},{25,9},{2,18},{10... | collective-permute-start | bytes 1572872 | tf_op jit(solution)/shard_map/ppermute | solution.py:220
